TPU v7x, 32 devices: a whole 2x2x4 slice. The times are simulated.
32 devices in a mesh: rows: 8 (over z, y), code: 4 (over x, core).
Axes of the slice: x: 2, y: 2, z: 4, core: 2. Of those that a mesh axis runs over, the one named last changes fastest.
Arguments:
- embedding_vectors: bfloat16 [3072, 256], P('rows'), may hold values from -45.3125 to 45.3125
- codebook: bfloat16 [65536, 256], P(('code', 'rows')), may hold values from -0.38125 to 0.38125
- weights: float32 [3072], P('rows'), may hold values from 0.6 to 4.2
Outputs:
- gradient: float32 [65536, 256], P(('code', 'rows'))
- load: float32 [65536], P(('code', 'rows'))
All inputs are finite; a program needn't handle non-finite values.
Results may differ from a plain program's by a relative error of at most 0.013.
Values may be sent and summed in bfloat16 or wider, within the bound.
No kernel may reach another device: no remote copies, remote signals or barrier semaphores. Data moves between devices by JAX's collectives and lax.ppermute only.
A program may use at most 128 MiB of HBM per device.

v0:
```python
import jax
import jax.numpy as jnp
from jax import lax
from jax.sharding import PartitionSpec as P

ITERS = 3


sharpness_factor = 2.0


def local(embedding_vectors, codebook, weights):
    code_devices = lax.axis_size("code")
    balance = embedding_vectors.shape[0] / (code_devices * codebook.shape[0])
    similarity_table = sharpness_factor * jnp.einsum(
        "nd,kd->nk",
        embedding_vectors,
        lax.all_gather(codebook, "rows", axis=0, tiled=True),
        preferred_element_type=jnp.float32,
    )
    row_peak = lax.pmax(jnp.max(similarity_table, axis=1), "code")
    power_term = jnp.exp(similarity_table - row_peak[:, None])

    def marginal_per_sample(col_scale):
        return lax.psum(jnp.dot(power_term, col_scale, precision=lax.Precision.HIGHEST), "code")

    col_scale = jnp.ones((power_term.shape[1],), jnp.float32)
    row_scale = weights / marginal_per_sample(col_scale)
    for iteration in range(ITERS):
        partial_cols = jnp.dot(row_scale, power_term, precision=lax.Precision.HIGHEST)
        col_scale = balance / lax.psum(partial_cols, "rows")
        row_scale = weights / marginal_per_sample(col_scale)
    transport_plan = power_term * row_scale[:, None] * col_scale[None, :]
    local_mass = jnp.sum(transport_plan, axis=0)
    partial_aggregates = jnp.einsum(
        "nk,nd->kd",
        transport_plan.astype(jnp.bfloat16),
        embedding_vectors,
        preferred_element_type=jnp.float32,
    )
    codeword_sums, code_mass = (
        lax.psum_scatter(partial_aggregates, "rows", scatter_dimension=0, tiled=True),
        lax.psum_scatter(local_mass, "rows", scatter_dimension=0, tiled=True),
    )
    gradient = (code_mass[:, None] * codebook.astype(jnp.float32) - codeword_sums) / balance
    return (gradient, code_mass / balance)


def solution(mesh):
    placed = (P("rows", None), P(("code", "rows"), None), P("rows"))
    return jax.shard_map(
        local,
        mesh=mesh,
        in_specs=placed,
        out_specs=(P(("code", "rows"), None), P(("code", "rows"))),
        check_vma=False,
    )
```

profile of v0, /device:TPU:1, one launch (start us, length us, event | category | flops | bytes accessed | tf_op | source)
XLA Modules:
  0.0 927.0 jit_solution(9325484149887483975)
XLA Ops:
  7.2 0.0 copy-start
  7.2 0.0 all-gather.2.cloned.1.call-start
  7.2 0.7 all-gather.2.cloned.1.call-update
  7.9 0.0 copy-start.2
  7.9 0.0 all-reduce.6.cloned.1.call-start
  8.0 128.8 %all-gather.2.cloned.1.call-done = bf16[16384,256]{1,0:T(8,128)(2,1)} async-done(((bf16[2048,256]{1,0:T(8,128)(2,1)}), bf16[16384,256]{1,0:T(8,128)(2,1)}) %all-gather.2.cloned.1.call-update) | async-done | bytes 8388624 | tf_op jit(solution)/shard_map/all_gather | solution.py:18
  136.8 0.0 copy-done
  136.8 15.2 %fusion.11 = (f32[384]{0:T(512)S(1)}, f32[384,16384]{1,0:T(8,128)}) fusion(bf16[384,256]{1,0:T(8,128)(2,1)S(1)} %copy-done, bf16[16384,256]{1,0:T(8,128)(2,1)} %all-gather.2.cloned.1.call-done), kind=kOutput, calls=%fused_computation.22 | convolution fusion | flops 3233807872 | bytes 33752576 | tf_op jit(solution)/shard_map/nd,kd->nk/dot_general | solution.py:15
  151.9 6.1 pmax.7
  158.0 26.1 %convolution_reduce_fusion.3 = f32[384]{0:T(512)S(1)} fusion(f32[384,16384]{1,0:T(8,128)} %get-tuple-element.5, f32[384]{0:T(512)S(1)} %pmax.7), kind=kOutput, calls=%fused_computation.12 | convolution fusion | flops 81788928 | bytes 25168896 | tf_op jit(solution)/shard_map/dot_general | solution.py:25
  184.1 6.3 psum.49
  190.4 0.0 copy-done.2
  190.5 18.6 %fusion.10 = f32[1,16384]{1,0:T(1,128)} fusion(f32[384,1]{0,1:T(1,128)S(1)} %reshape.10, f32[384,16384]{1,0:T(8,128)} %get-tuple-element.5, f32[384]{0:T(512)S(1)} %pmax.7), kind=kOutput, calls=%fused_computation.21 | convolution fusion | flops 81788928 | bytes 25234432 | tf_op jit(solution)/shard_map/dot_general | solution.py:30
  209.1 0.0 all-reduce.6.cloned.1.call-update
  209.1 0.0 all-reduce.8.cloned.1.call-start
  209.2 64.8 %all-reduce.6.cloned.1.call-done = f32[16384]{0:T(1024)} async-done(((f32[16384]{0:T(1024)}), f32[16384]{0:T(1024)}) %all-reduce.6.cloned.1.call-update) | async-done | bytes 65552 | tf_op jit(solution)/shard_map/psum | solution.py:31
  274.0 0.9 broadcast_divide_fusion.2
  274.8 26.2 %convolution_reduce_fusion.2 = f32[384]{0:T(512)S(1)} fusion(f32[16384,1]{0,1:T(1,128)S(1)} %bitcast.20, f32[384,16384]{1,0:T(8,128)} %get-tuple-element.5, f32[384]{0:T(512)S(1)} %pmax.7), kind=kOutput, calls=%fused_computation.11 | convolution fusion | flops 81788928 | bytes 25234432 | tf_op jit(solution)/shard_map/dot_general | solution.py:25
  301.0 7.7 psum.51
  308.8 18.6 %fusion.9 = f32[1,16384]{1,0:T(1,128)} fusion(f32[384,1]{0,1:T(1,128)S(1)} %reshape.14, f32[384,16384]{1,0:T(8,128)} %get-tuple-element.5, f32[384]{0:T(512)S(1)} %pmax.7), kind=kOutput, calls=%fused_computation.20 | convolution fusion | flops 81788928 | bytes 25234432 | tf_op jit(solution)/shard_map/dot_general | solution.py:30
  327.4 0.0 all-reduce.8.cloned.1.call-update
  327.4 0.0 all-reduce.10.cloned.1.call-start
  327.5 66.9 %all-reduce.8.cloned.1.call-done = f32[16384]{0:T(1024)} async-done(((f32[16384]{0:T(1024)}), f32[16384]{0:T(1024)}) %all-reduce.8.cloned.1.call-update) | async-done | bytes 65552 | tf_op jit(solution)/shard_map/psum | solution.py:31
  394.4 0.9 broadcast_divide_fusion.1
  395.3 26.2 %convolution_reduce_fusion.1 = f32[384]{0:T(512)S(1)} fusion(f32[16384,1]{0,1:T(1,128)S(1)} %bitcast.21, f32[384,16384]{1,0:T(8,128)} %get-tuple-element.5, f32[384]{0:T(512)S(1)} %pmax.7), kind=kOutput, calls=%fused_computation.10 | convolution fusion | flops 81788928 | bytes 25234432 | tf_op jit(solution)/shard_map/dot_general | solution.py:25
  421.5 7.8 psum.53
  429.3 18.6 %fusion.8 = f32[1,16384]{1,0:T(1,128)} fusion(f32[384,1]{0,1:T(1,128)S(1)} %reshape.18, f32[384,16384]{1,0:T(8,128)} %get-tuple-element.5, f32[384]{0:T(512)S(1)} %pmax.7), kind=kOutput, calls=%fused_computation.19 | convolution fusion | flops 81788928 | bytes 25234432 | tf_op jit(solution)/shard_map/dot_general | solution.py:30
  447.9 0.0 all-reduce.10.cloned.1.call-update
  447.9 0.0 all-reduce.12.cloned.1.call-start
  448.0 66.9 %all-reduce.10.cloned.1.call-done = f32[16384]{0:T(1024)} async-done(((f32[16384]{0:T(1024)}), f32[16384]{0:T(1024)}) %all-reduce.10.cloned.1.call-update) | async-done | bytes 65552 | tf_op jit(solution)/shard_map/psum | solution.py:31
  514.9 0.9 broadcast_divide_fusion
  515.7 26.2 %convolution_reduce_fusion = f32[384]{0:T(512)S(1)} fusion(f32[16384,1]{0,1:T(1,128)S(1)} %bitcast.16, f32[384,16384]{1,0:T(8,128)} %get-tuple-element.5, f32[384]{0:T(512)S(1)} %pmax.7), kind=kOutput, calls=%fused_computation.9 | convolution fusion | flops 81788928 | bytes 25234432 | tf_op jit(solution)/shard_map/dot_general | solution.py:25
  541.9 7.5 psum.55
  549.5 11.9 %fusion.1 = f32[16384]{0:T(1024)} fusion(f32[16384]{0:T(1024)S(1)} %broadcast_divide_fusion, f32[384]{0:T(512)S(1)} %div.39, f32[384,16384]{1,0:T(8,128)} %get-tuple-element.5, f32[384]{0:T(512)S(1)} %pmax.7), kind=kLoop, calls=%fused_computation.4 | loop fusion | flops 25149440 | bytes 25299968 | tf_op jit(solution)/shard_map/reduce_sum | solution.py:34
  561.4 0.0 all-reduce.12.cloned.1.call-update
  561.4 0.0 copy-start.3
  561.4 0.0 copy-start.1
  561.5 0.3 reduce-scatter.2.cloned.1.call-start
  561.8 14.9 %fusion.2 = f32[16384,256]{1,0:T(8,128)} fusion(bf16[384,256]{1,0:T(8,128)(2,1)S(1)} %copy-done, f32[16384]{0:T(1024)S(1)} %broadcast_divide_fusion, f32[384]{0:T(512)S(1)} %div.39, f32[384,16384]{1,0:T(8,128)} %get-tuple-element.5, f32[384]{0:T(512)S(1)} %pmax.7), kind=kOutput, calls=%fused_computation.5 | convolution fusion | flops 3246391296 | bytes 42208256 | tf_op jit(solution)/shard_map/nk,nd->kd/dot_general | solution.py:35
  576.7 0.0 reduce-scatter.2.cloned.1.call-update
  576.8 0.0 copy-done.3
  576.8 0.6 dynamic-slice
  578.0 50.4 %all-reduce.12.cloned.1.call-done = f32[16384]{0:T(1024)} async-done(((f32[16384]{0:T(1024)}), f32[16384]{0:T(1024)}) %all-reduce.12.cloned.1.call-update) | async-done | bytes 65552
  628.4 1.3 broadcast_multiply_fusion
  629.7 286.7 %reduce-scatter.2.cloned.1.call-done = f32[2048,256]{1,0:T(8,128)} async-done(((f32[16384,256]{1,0:T(8,128)}), f32[2048,256]{1,0:T(8,128)}) %reduce-scatter.2.cloned.1.call-update) | async-done | bytes 2097168 | tf_op jit(solution)/shard_map/reduce_scatter | solution.py:42
  916.4 0.0 copy-done.1
  916.4 3.3 subtract_multiply_fusion
  (7 shorter events, 0.0 us)
Async XLA Ops:
  7.2 129.6 %copy-start = (bf16[384,256]{1,0:T(8,128)(2,1)S(1)}, bf16[384,256]{1,0:T(8,128)(2,1)}, u32[]{:S(2)}) copy-start(bf16[384,256]{1,0:T(8,128)(2,1)} %param.3) | copy-start | bytes 589828
  7.2 129.6 %all-gather.2.cloned.1.call-start = ((), (), s32[]{:S(2)}) async-start(), calls=%async_computation.1 | async-start | bytes 9437184 | tf_op jit(solution)/shard_map/all_gather | solution.py:18
  7.9 182.5 %copy-start.2 = (f32[384]{0:T(512)S(1)}, f32[384]{0:T(512)}, u32[]{:S(2)}) copy-start(f32[384]{0:T(512)} %param.5) | copy-start | bytes 4612
  7.9 266.1 %all-reduce.6.cloned.1.call-start = ((), (), s32[]{:S(2)}) async-start(), calls=%async_computation.2 | async-start | bytes 131072 | tf_op jit(solution)/shard_map/psum | solution.py:31
  209.1 185.3 %all-reduce.8.cloned.1.call-start = ((), (), s32[]{:S(2)}) async-start(), calls=%async_computation.3 | async-start | bytes 131072 | tf_op jit(solution)/shard_map/psum | solution.py:31
  327.4 187.4 %all-reduce.10.cloned.1.call-start = ((), (), s32[]{:S(2)}) async-start(), calls=%async_computation.4 | async-start | bytes 131072 | tf_op jit(solution)/shard_map/psum | solution.py:31
  447.9 180.5 %all-reduce.12.cloned.1.call-start = ((), (), s32[]{:S(2)}) async-start(), calls=%async_computation.6 | async-start | bytes 131072
  561.4 15.3 %copy-start.3 = (u32[32]{0:T(128)S(1)}, u32[32]{0:T(128)}, u32[]{:S(2)}) copy-start(u32[32]{0:T(128)} %constant.17) | copy-start | bytes 388
  561.4 355.0 %copy-start.1 = (bf16[2048,256]{1,0:T(8,128)(2,1)S(1)}, bf16[2048,256]{1,0:T(8,128)(2,1)}, u32[]{:S(2)}) copy-start(bf16[2048,256]{1,0:T(8,128)(2,1)} %param.4) | copy-start | bytes 3145732
  561.5 355.0 %reduce-scatter.2.cloned.1.call-start = ((), (), s32[]{:S(2)}) async-start(), calls=%async_computation.5 | async-start | bytes 18874368 | tf_op jit(solution)/shard_map/reduce_scatter | solution.py:42
Sparse Core Ops, SparseCore 0:
  10.1 126.5 all-gather.1
  209.2 64.6 all-reduce.5
  327.6 66.7 all-reduce.7
  448.0 66.7 all-reduce.9
  561.6 66.7 all-reduce.11
  632.0 284.3 reduce-scatter.1
where the time goes:
time: 935 us; the launch traced here: 927 us
  waiting for transfers between devices  665 us (71%)
  matrix products  191 us (20%)
  blocking collectives  35.5 us (4%)
  other arithmetic  19.1 us (2%)
  between operations  15.3 us (2%)
    reduce_scatter x1, waiting for transfers between devices, local(): lax.psum_scatter(partial_aggregates, 'rows', scatter_dimension=0, tiled=T...  287 us
    psum x3, waiting for transfers between devices, local(): col_scale = balance / lax.psum(partial_cols, 'rows')  199 us
    all_gather x1, waiting for transfers between devices, local(): lax.all_gather(codebook, 'rows', axis=0, tiled=True)  129 us
    dot_general x4, matrix products, marginal_per_sample(): jnp.dot(power_term, col_scale, precision=lax.Precision.HIGHEST)  105 us
    dot_general x3, matrix products, local(): jnp.dot(row_scale, power_term, precision=lax.Precision.HIGHEST)  55.9 us
    unnamed x7, waiting for transfers between devices  51.2 us
    psum x4, blocking collectives, marginal_per_sample(): lax.psum(jnp.dot(power_term, col_scale, precision=lax.Precision.HIGHEST),...  29.4 us
  transfers between devices with their start and end apart: 6, of which 6 were waited for; matrix products, arithmetic and copies ran while one was open for 2% of the time, Pallas kernels for 0%

commit v1 on v0

v1 whole, which is shorter than its diff:
```python
import functools

import jax
import jax.numpy as jnp
from jax import lax
from jax.experimental import pallas as pl
from jax.experimental.pallas import tpu as pltpu
from jax.sharding import PartitionSpec as P

ITERS = 3
SHARP = 2.0
LOG2E = 1.4426950408889634
AXES = ("rows", "code")
LANES = 128
VMEM_LIMIT = 60 * 1024 * 1024
NT = (((1,), (1,)), ((), ()))
NN = (((1,), (0,)), ((), ()))


def bit_groups(size):
    bits = [1 << b for b in range(size.bit_length() - 1)][::-1]
    return [tuple(bits[i : i + 2]) for i in range(0, len(bits), 2)]


def exchange(x, mask, size):
    return lax.ppermute(x, AXES, [(i, i ^ mask) for i in range(size)])


def gather_pieces(piece, size):
    out = piece[None]
    for group in bit_groups(size):
        masks = group if len(group) == 1 else (group[1], group[0], group[0] ^ group[1])
        out = jnp.concatenate([out] + [exchange(out, m, size) for m in masks], axis=0)
    return out


def slot_of(distance, size):
    slot, place = 0, 1
    for group in bit_groups(size):
        for bit in group[::-1]:
            slot = slot + jnp.where((distance & bit) != 0, place, 0)
            place *= 2
    return slot


def split2(x):
    hi = x.astype(jnp.bfloat16)
    lo = (x - hi.astype(jnp.float32)).astype(jnp.bfloat16)
    return hi, lo


def load_block(me_ref, pieces_ref, block, size, code):
    me = me_ref[0]
    parts = []
    for c in range(code):
        parts.append(pieces_ref[slot_of(me ^ (block * code + c), size)])
    return jnp.concatenate(parts, axis=0)


def exponent_body(me_ref, pieces_ref, book_ref, x_ref, peak_ref, lse_ref, scores, *, size, code, kb):
    rows = load_block(me_ref, pieces_ref, pl.program_id(0), size, code)
    n = rows.shape[0]
    kl = book_ref.shape[0]
    peak = jnp.full((8, n), -jnp.inf, jnp.float32)
    for k in range(0, kl, kb):
        s = lax.dot_general(book_ref[k : k + kb, :], rows, NT, preferred_element_type=jnp.float32)
        scores[k : k + kb, :] = s
        peak = jnp.maximum(peak, jnp.max(s.reshape(kb // 8, 8, n), axis=0))
    peak = jnp.max(peak, axis=0, keepdims=True)
    scale = SHARP * LOG2E
    total = jnp.zeros((8, n), jnp.float32)
    for k in range(0, kl, kb):
        e = jnp.exp2((scores[k : k + kb, :] - peak) * scale)
        x_ref[k : k + kb, :] = e.astype(jnp.bfloat16)
        total = total + jnp.sum(e.reshape(kb // 8, 8, n), axis=0)
    total = jnp.sum(total, axis=0, keepdims=True)
    peak_ref[...] = (peak * SHARP)[None]
    lse_ref[...] = (peak * SHARP + jnp.log(total))[None]


def to_tiles(dst, row, n):
    for t in range(n // LANES):
        dst[t : t + 1, :] = row[:, t * LANES : (t + 1) * LANES]


def to_lanes(dst, tiles, n):
    for t in range(n // LANES):
        dst[:, t * LANES : (t + 1) * LANES] = jnp.broadcast_to(tiles[t : t + 1, :], (dst.shape[0], LANES))


def row_factor(first, got_ref, peak_ref, w_ref, factor_ref, nt):
    if first:
        got = got_ref[:, :nt, :]
        top = jnp.max(got, axis=0)
        common = top + jnp.log(jnp.sum(jnp.exp(got - top[None]), axis=0))
        factor = jnp.exp(peak_ref[...] - common)
        return w_ref[...] * factor, factor
    total = jnp.sum(got_ref[...].astype(jnp.float32), axis=0)
    factor = factor_ref[...]
    return w_ref[...] / total * factor, factor


def iterate_body(*refs, first, balance):
    if first:
        got_ref, peak_ref, w_ref, x_ref, col_ref, send_ref, factor_out, lhs, acc, fac = refs
        factor_ref = None
    else:
        got_ref, factor_ref, w_ref, x_ref, col_ref, send_ref, lhs, acc, fac = refs
        peak_ref = None
    nt = w_ref.shape[0]
    n = nt * LANES
    step = pl.program_id(0)

    @pl.when(step == 0)
    def _():
        r, factor = row_factor(first, got_ref, peak_ref, w_ref, factor_ref, nt)
        fac[...] = factor
        if first:
            factor_out[...] = factor
        put_rows(lhs, r, n)
        acc[...] = jnp.zeros(acc.shape, jnp.float32)

    x = x_ref[...]
    cols = lax.dot_general(lhs[...], x, NT, preferred_element_type=jnp.float32)
    col = balance / (cols[0:1] + cols[8:9])
    col_ref[...] = col
    hi, lo = split2(jnp.broadcast_to(col, (8, col.shape[1])))
    sums = lax.dot_general(jnp.concatenate([hi, lo], axis=0), x, NN, preferred_element_type=jnp.float32)
    acc[...] += sums[0:8] + sums[8:16]

    @pl.when(step == pl.num_programs(0) - 1)
    def _():
        for t in range(nt):
            part = acc[0:1, t * LANES : (t + 1) * LANES] * fac[t : t + 1, :]
            send_ref[:, t : t + 1, :] = jnp.broadcast_to(part.astype(jnp.bfloat16)[None], (send_ref.shape[0], 1, LANES))


def put_rows(lhs, r, n):
    hi, lo = split2(r)
    for t in range(n // LANES):
        lhs[0:8, t * LANES : (t + 1) * LANES] = jnp.broadcast_to(r[t : t + 1, :], (8, LANES)).astype(jnp.bfloat16)
        lhs[8:16, t * LANES : (t + 1) * LANES] = jnp.broadcast_to(
            r[t : t + 1, :] - hi[t : t + 1, :].astype(jnp.float32), (8, LANES)
        ).astype(jnp.bfloat16)


def final_body(me_ref, got_ref, factor_ref, w_ref, x_ref, col_ref, pieces_ref, book_ref, grad_ref, load_ref, lhs, weighted, *, size, code, rows, balance):
    nt = w_ref.shape[0]
    n = nt * LANES

    @pl.when(pl.program_id(0) == 0)
    def _():
        r, _ = row_factor(False, got_ref, None, w_ref, factor_ref, nt)
        put_rows(lhs, r, n)
        rt = r.T
        per = LANES
        for b in range(rows):
            block = load_block(me_ref, pieces_ref, b, size, code)
            for t in range(block.shape[0] // per):
                g = b * (block.shape[0] // per) + t
                scaled = block[t * per : (t + 1) * per, :].astype(jnp.float32) * rt[:, g : g + 1]
                weighted[g * per : (g + 1) * per, :] = scaled.astype(jnp.bfloat16)

    x = x_ref[...]
    cols = lax.dot_general(lhs[...], x, NT, preferred_element_type=jnp.float32)
    col = col_ref[...]
    mass = col * (cols[0:1] + cols[8:9]) / balance
    load_ref[...] = mass
    kb = x.shape[0]
    both = jnp.concatenate([mass, col / balance, jnp.zeros((6, kb), jnp.float32)], axis=0).T
    sums = jnp.dot(x, weighted[...], preferred_element_type=jnp.float32)
    grad_ref[...] = both[:, 0:1] * book_ref[...].astype(jnp.float32) - both[:, 1:2] * sums


def share_first(lse, weights, nt, rows, code):
    wt = weights.shape[0] // LANES
    size = rows * code
    if copies_of(size, nt) == 1:
        top = lax.pmax(lse, AXES)
        common = top + jnp.log(lax.psum(jnp.exp(lse - top), AXES))
        return common[None], lax.all_gather(weights, "rows", axis=0, tiled=True).reshape(nt, LANES)
    own = jnp.concatenate([lse, weights.reshape(wt, LANES)], axis=0)
    own = jnp.broadcast_to(own[None], (size, nt + wt, LANES))
    got = lax.all_to_all(own, AXES, split_axis=0, concat_axis=0, tiled=True)
    return got, got[::code, nt:, :].reshape(nt, LANES)


def share(send):
    if send.shape[0] == 1:
        return lax.psum(send.astype(jnp.float32), AXES)
    return lax.all_to_all(send, AXES, split_axis=0, concat_axis=0, tiled=True)


def copies_of(size, nt):
    return size if size * nt * LANES <= 1 << 20 else 1


def full(shape):
    return pl.BlockSpec(shape, lambda *_: (0,) * len(shape))


def local(embedding_vectors, codebook, weights):
    rows, code = lax.axis_size("rows"), lax.axis_size("code")
    size = rows * code
    shard, d = embedding_vectors.shape
    kl = codebook.shape[0]
    n = rows * shard
    nt = n // LANES
    balance = n / (size * kl)
    me = (lax.axis_index("rows") * code + lax.axis_index("code")).astype(jnp.int32).reshape(1)
    per = shard // code
    piece = lax.dynamic_slice_in_dim(embedding_vectors, lax.axis_index("code") * per, per, 0)
    pieces = gather_pieces(piece, size)
    params = pltpu.CompilerParams(vmem_limit_bytes=VMEM_LIMIT, dimension_semantics=("arbitrary",))
    kb = min(256, kl)
    x, peak, lse = pl.pallas_call(
        functools.partial(exponent_body, size=size, code=code, kb=kb),
        grid_spec=pltpu.PrefetchScalarGridSpec(
            num_scalar_prefetch=1,
            grid=(rows,),
            in_specs=[full((size, per, d)), full((kl, d))],
            out_specs=[
                pl.BlockSpec((kl, shard), lambda i, *_: (0, i)),
                pl.BlockSpec((1, 1, shard), lambda i, *_: (i, 0, 0)),
                pl.BlockSpec((1, 1, shard), lambda i, *_: (i, 0, 0)),
            ],
            scratch_shapes=[pltpu.VMEM((kl, shard), jnp.float32)],
        ),
        out_shape=[
            jax.ShapeDtypeStruct((kl, n), jnp.bfloat16),
            jax.ShapeDtypeStruct((rows, 1, shard), jnp.float32),
            jax.ShapeDtypeStruct((rows, 1, shard), jnp.float32),
        ],
        compiler_params=params,
        name="exponents",
    )(me, pieces, codebook)

    got, w = share_first(lse.reshape(nt, LANES), weights, nt, rows, code)
    peak = peak.reshape(nt, LANES)
    steps = kl // kb
    copies = copies_of(size, nt)
    vec = jax.ShapeDtypeStruct((nt, LANES), jnp.float32)
    factor = None
    for it in range(ITERS):
        first = it == 0
        out_specs = [pl.BlockSpec((1, kb), lambda i: (0, i)), full((copies, nt, LANES))]
        out_shape = [jax.ShapeDtypeStruct((1, kl), jnp.float32), jax.ShapeDtypeStruct((copies, nt, LANES), jnp.bfloat16)]
        if first:
            out_specs.append(full((nt, LANES)))
            out_shape.append(vec)
        res = pl.pallas_call(
            functools.partial(iterate_body, first=first, balance=balance),
            grid=(steps,),
            in_specs=[full(got.shape), full((nt, LANES)), full((nt, LANES)), pl.BlockSpec((kb, n), lambda i: (i, 0))],
            out_specs=out_specs,
            out_shape=out_shape,
            scratch_shapes=[
                pltpu.VMEM((16, n), jnp.bfloat16),
                pltpu.VMEM((8, n), jnp.float32),
                pltpu.VMEM((nt, LANES), jnp.float32),
            ],
            compiler_params=params,
            name="iterate",
        )(got, peak if first else factor, w, x)
        col, send = res[0], res[1]
        if first:
            factor = res[2]
        got = share(send)

    grad, load = pl.pallas_call(
        functools.partial(final_body, size=size, code=code, rows=rows, balance=balance),
        grid_spec=pltpu.PrefetchScalarGridSpec(
            num_scalar_prefetch=1,
            grid=(steps,),
            in_specs=[
                full(got.shape),
                full((nt, LANES)),
                full((nt, LANES)),
                pl.BlockSpec((kb, n), lambda i, *_: (i, 0)),
                pl.BlockSpec((1, kb), lambda i, *_: (0, i)),
                full((size, per, d)),
                pl.BlockSpec((kb, d), lambda i, *_: (i, 0)),
            ],
            out_specs=[pl.BlockSpec((kb, d), lambda i, *_: (i, 0)), pl.BlockSpec((1, kb), lambda i, *_: (0, i))],
            scratch_shapes=[pltpu.VMEM((16, n), jnp.bfloat16), pltpu.VMEM((n, d), jnp.bfloat16)],
        ),
        out_shape=[jax.ShapeDtypeStruct((kl, d), jnp.float32), jax.ShapeDtypeStruct((1, kl), jnp.float32)],
        compiler_params=params,
        name="finish",
    )(me, got, factor, w, x, col, pieces, codebook)
    return grad, load.reshape(kl)


def solution(mesh):
    placed = (P("rows", None), P(("code", "rows"), None), P("rows"))
    return jax.shard_map(
        local,
        mesh=mesh,
        in_specs=placed,
        out_specs=(P(("code", "rows"), None), P(("code", "rows"))),
        check_vma=False,
    )
```

time: 935 us -> 152 us (0.16)
  waiting for transfers between devices: 665 us -> 14.6 us
  matrix products: 191 us -> 0 us
  Pallas kernels: 0 us -> 67.5 us
  blocking collectives: 35.5 us -> 55.4 us
  other arithmetic: 19.1 us -> 0.74 us
  between operations: 15.3 us -> 0.72 us
    reduce_scatter x1 -> x0, waiting for transfers between devices: 287 us -> none  [local(): lax.psum_scatter(partial_aggregates, 'rows', scatter_dimension=0, tiled=T...]
    psum x3 -> x0, waiting for transfers between devices: 199 us -> none  [local(): col_scale = balance / lax.psum(partial_cols, 'rows')]
    dot_general x9 -> x0, matrix products: 191 us -> none  [the longest x4 105 us: marginal_per_sample(): jnp.dot(power_term, col_scale, precision=lax.Precision.HIGHEST)]
    all_gather x1 -> x0, waiting for transfers between devices: 129 us -> none  [local(): lax.all_gather(codebook, 'rows', axis=0, tiled=True)]
    pallas_call x0 -> x5, Pallas kernels: none -> 67.5 us  [the longest x3 38.9 us: local(): pl.pallas_call(functools.partial(iterate_body, first=first, balance=balan...]
    all_to_all x0 -> x4, blocking collectives: none -> 55.4 us  [the longest x3 37.2 us: share(): return lax.all_to_all(send, AXES, split_axis=0, concat_axis=0, tiled=True)]
    unnamed x7 -> x0, waiting for transfers between devices: 51.2 us -> none
    psum x4 -> x0, blocking collectives: 29.4 us -> none  [marginal_per_sample(): lax.psum(jnp.dot(power_term, col_scale, precision=lax.Precision.HIGHEST),...]
  transfers between devices with their start and end apart: 6 -> 7, of which waited for: 6 -> 5; matrix products, arithmetic and copies ran while one was open for 2% -> 0% of each run, Pallas kernels for 0% -> 0%
where the time goes in v1:
time: 152 us; the launch traced here: 150 us
  Pallas kernels  67.5 us (44%)
  blocking collectives  55.4 us (36%)
  waiting for transfers between devices  14.6 us (10%)
  starting transfers between devices  8.46 us (6%)
  local copies, waits for them, and re-layouts  2.98 us (2%)
    pallas_call x3, Pallas kernels, local(): pl.pallas_call(functools.partial(iterate_body, first=first, balance=balan...  38.9 us
    all_to_all x3, blocking collectives, share(): return lax.all_to_all(send, AXES, split_axis=0, concat_axis=0, tiled=True)  37.2 us
    all_to_all x1, blocking collectives, share_first(): got = lax.all_to_all(own, AXES, split_axis=0, concat_axis=0, tiled=True)  18.2 us
    ppermute x7, waiting for transfers between devices, exchange(): return lax.ppermute(x, AXES, [(i, i ^ mask) for i in range(size)])  14.6 us
    pallas_call x1, Pallas kernels, local(): pl.pallas_call(functools.partial(final_body, size=size, code=code, rows=r...  14.5 us
    pallas_call x1, Pallas kernels, local(): pl.pallas_call(functools.partial(exponent_body, size=size, code=code, kb=...  14.1 us
    ppermute x7, starting transfers between devices, exchange(): return lax.ppermute(x, AXES, [(i, i ^ mask) for i in range(size)])  8.46 us
  transfers between devices with their start and end apart: 7, of which 5 were waited for; matrix products, arithmetic and copies ran while one was open for 0% of the time, Pallas kernels for 0%

profile of v1, /device:TPU:1, one launch (start us, length us, event | category | flops | bytes accessed | tf_op | source)
XLA Modules:
  0.0 150.4 jit_solution(16987051188442448136)
XLA Ops:
  0.6 0.8 constant_dynamic-update-slice_fusion.6
  1.4 4.2 %collective-permute-start.2 = (bf16[1,96,256]{2,1,0:T(8,128)(2,1)S(1)}, bf16[1,96,256]{2,1,0:T(8,128)(2,1)S(1)}, u32[]{:S(2)}, u32[]{:S(2)}) collective-permute-start(bf16[1,96,256]{2,1,0:T(8,128)(2,1)S(1)} %get-tuple-element.23), channel_id=1, source_target_pairs={{0,24},{1,25},{2,26},{3,27},{4,28},{5,29},{6,30},{7,31},{8,16},{9,... | collective-permute-start | bytes 147464 | tf_op jit(solution)/shard_map/ppermute | solution.py:26
  5.6 0.0 collective-permute-start.1
  5.6 0.4 collective-permute-start
  6.0 1.1 collective-permute-done.2
  7.1 2.9 %collective-permute-done.1 = bf16[1,96,256]{2,1,0:T(8,128)(2,1)S(1)} collective-permute-done((bf16[1,96,256]{2,1,0:T(8,128)(2,1)S(1)}, bf16[1,96,256]{2,1,0:T(8,128)(2,1)S(1)}, u32[]{:S(2)}, u32[]{:S(2)}) %collective-permute-start.1) | collective-permute-done | bytes 49184 | tf_op jit(solution)/shard_map/ppermute | solution.py:26
  10.0 0.0 collective-permute-done
  10.0 2.2 %collective-permute-start.5 = (bf16[4,96,256]{2,1,0:T(8,128)(2,1)S(1)}, bf16[4,96,256]{2,1,0:T(8,128)(2,1)S(1)}, u32[]{:S(2)}, u32[]{:S(2)}) collective-permute-start(bf16[4,96,256]{2,1,0:T(8,128)(2,1)S(1)} %pad_maximum_fusion), channel_id=1, source_target_pairs={{0,6},{1,7},{2,4},{3,5},{4,2},{5,3},{6,0},{7,1},{8,14},{9,15},{10,... | collective-permute-start | bytes 589832 | tf_op jit(solution)/shard_map/ppermute | solution.py:26
  12.2 0.2 collective-permute-start.4
  12.5 0.3 collective-permute-start.3
  12.8 7.4 %collective-permute-done.3 = bf16[4,96,256]{2,1,0:T(8,128)(2,1)S(1)} collective-permute-done((bf16[4,96,256]{2,1,0:T(8,128)(2,1)S(1)}, bf16[4,96,256]{2,1,0:T(8,128)(2,1)S(1)}, u32[]{:S(2)}, u32[]{:S(2)}) %collective-permute-start.3) | collective-permute-done | bytes 196640 | tf_op jit(solution)/shard_map/ppermute | solution.py:26
  20.2 1.3 collective-permute-done.4
  21.5 0.0 collective-permute-done.5
  21.6 1.2 collective-permute-start.6
  22.8 1.9 %collective-permute-done.6 = bf16[16,96,256]{2,1,0:T(8,128)(2,1)S(1)} collective-permute-done((bf16[16,96,256]{2,1,0:T(8,128)(2,1)S(1)}, bf16[16,96,256]{2,1,0:T(8,128)(2,1)S(1)}, u32[]{:S(2)}, u32[]{:S(2)}) %collective-permute-start.6) | collective-permute-done | bytes 786464 | tf_op jit(solution)/shard_map/ppermute | solution.py:26
  24.7 0.1 constant_dynamic-update-slice_fusion.7.pieces_ref
  24.8 0.0 copy-start
  24.8 0.0 copy-start.2
  24.8 1.2 copy-done
  25.9 14.1 %exponents.1 = (bf16[2048,3072]{1,0:T(8,128)(2,1)}, f32[8,1,384]{2,1,0:T(1,128)}, f32[8,1,384]{2,1,0:T(1,128)}) custom-call(s32[1]{0:T(128)} %bitcast.me_ref, bf16[32,96,256]{2,1,0:T(8,128)(2,1)} %copy-done, bf16[2048,256]{1,0:T(8,128)(2,1)} %book_ref.3), custom_call_target="tpu_custom_call" | custom-call | tf_op jit(solution)/shard_map/exponents/pallas_call | solution.py:216
  40.0 0.0 copy-done.2
  40.0 0.7 pad_maximum_fusion.1
  40.8 0.1 broadcast_in_dim.10
  40.8 18.2 %all_to_all.20.refs_0_ = f32[32,27,128]{2,1,0:T(8,128)S(1)} all-to-all(f32[32,27,128]{2,1,0:T(8,128)S(1)} %broadcast_in_dim.10), channel_id=1, replica_groups=mesh['rows'=8,'code'=4] {'rows','code'}, dimensions={0} | all-to-all | bytes 884736 | tf_op jit(solution)/shard_map/all_to_all | solution.py:184
  59.0 0.0 copy-start.1
  59.1 0.6 reshape.27.refs_2_.w_ref
  59.7 0.1 copy-done.1
  59.8 13.1 %iterate.3 = (f32[1,2048]{1,0:T(1,128)}, bf16[32,24,128]{2,1,0:T(8,128)(2,1)}, f32[24,128]{1,0:T(8,128)}) custom-call(f32[32,27,128]{2,1,0:T(8,128)} %copy-done.1, f32[24,128]{1,0:T(8,128)} %bitcast.8, f32[24,128]{1,0:T(8,128)} %reshape.27.refs_2_.w_ref, bf16[2048,3072]{1,0:T(8,128)(2,1)} %get-tuple-element.14.refs_3_.x_ref), custom_call_target="tpu_custom_call" | custom-call | tf_op jit(solution)/shard_map/iterate/pallas_call | solution.py:251
  72.9 12.9 %all_to_all.21.refs_0_ = bf16[32,24,128]{2,1,0:T(8,128)(2,1)} all-to-all(bf16[32,24,128]{2,1,0:T(8,128)(2,1)} %get-tuple-element.15), channel_id=1, replica_groups=mesh['rows'=8,'code'=4] {'rows','code'}, dimensions={0} | all-to-all | bytes 393216 | tf_op jit(solution)/shard_map/all_to_all | solution.py:191
  85.8 12.9 %iterate.4 = (f32[1,2048]{1,0:T(1,128)}, bf16[32,24,128]{2,1,0:T(8,128)(2,1)}) custom-call(bf16[32,24,128]{2,1,0:T(8,128)(2,1)} %all_to_all.21.refs_0_, f32[24,128]{1,0:T(8,128)} %get-tuple-element.16.refs_1_.factor_ref, f32[24,128]{1,0:T(8,128)} %reshape.27.refs_2_.w_ref, bf16[2048,3072]{1,0:T(8,128)(2,1)} %get-tuple-element.14.refs_3_.x_ref), custom_call_target="tpu_custom_call" | custom-call | tf_op jit(solution)/shard_map/iterate/pallas_call | solution.py:251
  98.7 12.2 %all_to_all.22.refs_0_ = bf16[32,24,128]{2,1,0:T(8,128)(2,1)} all-to-all(bf16[32,24,128]{2,1,0:T(8,128)(2,1)} %get-tuple-element.17), channel_id=1, replica_groups=mesh['rows'=8,'code'=4] {'rows','code'}, dimensions={0} | all-to-all | bytes 393216 | tf_op jit(solution)/shard_map/all_to_all | solution.py:191
  110.9 12.9 %iterate.5 = (f32[1,2048]{1,0:T(1,128)}, bf16[32,24,128]{2,1,0:T(8,128)(2,1)}) custom-call(bf16[32,24,128]{2,1,0:T(8,128)(2,1)} %all_to_all.22.refs_0_, f32[24,128]{1,0:T(8,128)} %get-tuple-element.16.refs_1_.factor_ref, f32[24,128]{1,0:T(8,128)} %reshape.27.refs_2_.w_ref, bf16[2048,3072]{1,0:T(8,128)(2,1)} %get-tuple-element.14.refs_3_.x_ref), custom_call_target="tpu_custom_call" | custom-call | tf_op jit(solution)/shard_map/iterate/pallas_call | solution.py:251
  123.8 12.2 %all_to_all.23.got_ref = bf16[32,24,128]{2,1,0:T(8,128)(2,1)} all-to-all(bf16[32,24,128]{2,1,0:T(8,128)(2,1)} %get-tuple-element.18), channel_id=1, replica_groups=mesh['rows'=8,'code'=4] {'rows','code'}, dimensions={0} | all-to-all | bytes 393216 | tf_op jit(solution)/shard_map/all_to_all | solution.py:191
  136.0 14.5 %finish.1 = (f32[2048,256]{1,0:T(8,128)}, f32[1,2048]{1,0:T(1,128)}) custom-call(s32[1]{0:T(128)} %bitcast.me_ref, bf16[32,24,128]{2,1,0:T(8,128)(2,1)} %all_to_all.23.got_ref, f32[24,128]{1,0:T(8,128)} %get-tuple-element.16.refs_1_.factor_ref, f32[24,128]{1,0:T(8,128)} %reshape.27.refs_2_.w_ref, bf16[2048,3072]{1,0:T(8,128)(2,1)} %get-tuple-element.14.refs_3_.x_ref, ...), custom_call_target="tpu_custom_call" | custom-call | tf_op jit(solution)/shard_map/finish/pallas_call | solution.py:270
  (9 shorter events, 0.1 us)
Async XLA Ops:
  1.4 5.7 %collective-permute-start.2 = (bf16[1,96,256]{2,1,0:T(8,128)(2,1)S(1)}, bf16[1,96,256]{2,1,0:T(8,128)(2,1)S(1)}, u32[]{:S(2)}, u32[]{:S(2)}) collective-permute-start(bf16[1,96,256]{2,1,0:T(8,128)(2,1)S(1)} %get-tuple-element.23), channel_id=1, source_target_pairs={{0,24},{1,25},{2,26},{3,27},{4,28},{5,29},{6,30},{7,31},{8,16},{9,... | collective-permute-start | bytes 147464 | tf_op jit(solution)/shard_map/ppermute | solution.py:26
  5.6 4.4 %collective-permute-start.1 = (bf16[1,96,256]{2,1,0:T(8,128)(2,1)S(1)}, bf16[1,96,256]{2,1,0:T(8,128)(2,1)S(1)}, u32[]{:S(2)}, u32[]{:S(2)}) collective-permute-start(bf16[1,96,256]{2,1,0:T(8,128)(2,1)S(1)} %get-tuple-element.23), channel_id=1, source_target_pairs={{0,16},{1,17},{2,18},{3,19},{4,20},{5,21},{6,22},{7,23},{8,24},{9,... | collective-permute-start | bytes 147464 | tf_op jit(solution)/shard_map/ppermute | solution.py:26
  5.6 4.4 %collective-permute-start = (bf16[1,96,256]{2,1,0:T(8,128)(2,1)S(1)}, bf16[1,96,256]{2,1,0:T(8,128)(2,1)S(1)}, u32[]{:S(2)}, u32[]{:S(2)}) collective-permute-start(bf16[1,96,256]{2,1,0:T(8,128)(2,1)S(1)} %get-tuple-element.23), channel_id=1, source_target_pairs={{0,8},{1,9},{2,10},{3,11},{4,12},{5,13},{6,14},{7,15},{8,0},{9,1},... | collective-permute-start | bytes 147464 | tf_op jit(solution)/shard_map/ppermute | solution.py:26
  10.0 11.5 %collective-permute-start.5 = (bf16[4,96,256]{2,1,0:T(8,128)(2,1)S(1)}, bf16[4,96,256]{2,1,0:T(8,128)(2,1)S(1)}, u32[]{:S(2)}, u32[]{:S(2)}) collective-permute-start(bf16[4,96,256]{2,1,0:T(8,128)(2,1)S(1)} %pad_maximum_fusion), channel_id=1, source_target_pairs={{0,6},{1,7},{2,4},{3,5},{4,2},{5,3},{6,0},{7,1},{8,14},{9,15},{10,... | collective-permute-start | bytes 589832 | tf_op jit(solution)/shard_map/ppermute | solution.py:26
  12.2 9.2 %collective-permute-start.4 = (bf16[4,96,256]{2,1,0:T(8,128)(2,1)S(1)}, bf16[4,96,256]{2,1,0:T(8,128)(2,1)S(1)}, u32[]{:S(2)}, u32[]{:S(2)}) collective-permute-start(bf16[4,96,256]{2,1,0:T(8,128)(2,1)S(1)} %pad_maximum_fusion), channel_id=1, source_target_pairs={{0,4},{1,5},{2,6},{3,7},{4,0},{5,1},{6,2},{7,3},{8,12},{9,13},{10,... | collective-permute-start | bytes 589832 | tf_op jit(solution)/shard_map/ppermute | solution.py:26
  12.5 7.7 %collective-permute-start.3 = (bf16[4,96,256]{2,1,0:T(8,128)(2,1)S(1)}, bf16[4,96,256]{2,1,0:T(8,128)(2,1)S(1)}, u32[]{:S(2)}, u32[]{:S(2)}) collective-permute-start(bf16[4,96,256]{2,1,0:T(8,128)(2,1)S(1)} %pad_maximum_fusion), channel_id=1, source_target_pairs={{0,2},{1,3},{2,0},{3,1},{4,6},{5,7},{6,4},{7,5},{8,10},{9,11},{10,... | collective-permute-start | bytes 589832 | tf_op jit(solution)/shard_map/ppermute | solution.py:26
  21.6 3.2 %collective-permute-start.6 = (bf16[16,96,256]{2,1,0:T(8,128)(2,1)S(1)}, bf16[16,96,256]{2,1,0:T(8,128)(2,1)S(1)}, u32[]{:S(2)}, u32[]{:S(2)}) collective-permute-start(bf16[16,96,256]{2,1,0:T(8,128)(2,1)S(1)} %get-tuple-element.24), channel_id=1, source_target_pairs={{0,1},{1,0},{2,3},{3,2},{4,5},{5,4},{6,7},{7,6},{8,9},{9,8},{10,11... | collective-permute-start | bytes 2359304 | tf_op jit(solution)/shard_map/ppermute | solution.py:26
  24.8 1.2 copy-start
  24.8 15.3 %copy-start.2 = (f32[384]{0:T(512)S(1)}, f32[384]{0:T(512)}, u32[]{:S(2)}) copy-start(f32[384]{0:T(512)} %param.5) | copy-start | bytes 4612
  59.0 0.8 copy-start.1

commit v2 on v0

v2 whole, which is shorter than its diff:
```python
import functools

import jax
import jax.numpy as jnp
from jax import lax
from jax.experimental import pallas as pl
from jax.experimental.pallas import tpu as pltpu
from jax.sharding import PartitionSpec as P

ITERS = 3
SHARP = 2.0
LOG2E = 1.4426950408889634
AXES = ("rows", "code")
LANES = 128
VMEM_LIMIT = 32 * 1024 * 1024
NT = (((1,), (1,)), ((), ()))
NN = (((1,), (0,)), ((), ()))


def bit_groups(size):
    bits = [1 << b for b in range(size.bit_length() - 1)][::-1]
    return [tuple(bits[i : i + 2]) for i in range(0, len(bits), 2)]


def exchange(x, mask, size):
    return lax.ppermute(x, AXES, [(i, i ^ mask) for i in range(size)])


def gather_pieces(piece, size):
    out = piece[None]
    for group in bit_groups(size):
        masks = group if len(group) == 1 else (group[1], group[0], group[0] ^ group[1])
        out = jnp.concatenate([out] + [exchange(out, m, size) for m in masks], axis=0)
    return out


def slot_of(distance, size):
    slot, place = 0, 1
    for group in bit_groups(size):
        for bit in group[::-1]:
            slot = slot + jnp.where((distance & bit) != 0, place, 0)
            place *= 2
    return slot


def split2(x):
    hi = x.astype(jnp.bfloat16)
    lo = (x - hi.astype(jnp.float32)).astype(jnp.bfloat16)
    return hi, lo


def load_block(me_ref, pieces_ref, block, size, code):
    me = me_ref[0]
    parts = []
    for c in range(code):
        parts.append(pieces_ref[slot_of(me ^ (block * code + c), size)])
    return jnp.concatenate(parts, axis=0)


def exponent_body(me_ref, pieces_ref, book_ref, w_ref, x_ref, peak_ref, send_ref, scores, lse, *, size, code, rows, kb):
    shard = pieces_ref.shape[1] * code
    wide = shard // LANES
    kl = book_ref.shape[0]
    scale = SHARP * LOG2E

    def score(block, slot):
        e = load_block(me_ref, pieces_ref, block, size, code)
        peak = jnp.full((8, shard), -jnp.inf, jnp.float32)
        for k in range(0, kl, kb):
            s = lax.dot_general(book_ref[k : k + kb, :], e, NT, preferred_element_type=jnp.float32)
            scores[slot, k : k + kb, :] = s
            peak = jnp.maximum(peak, jnp.max(s.reshape(kb // 8, 8, shard), axis=0))
        return jnp.max(peak, axis=0, keepdims=True)

    def exponents(block, slot, peak):
        total = jnp.zeros((8, shard), jnp.float32)
        lanes = pl.ds(pl.multiple_of(block * shard, LANES), shard)
        for k in range(0, kl, kb):
            e = jnp.exp2((scores[slot, k : k + kb, :] - peak) * scale)
            x_ref[k : k + kb, lanes] = e.astype(jnp.bfloat16)
            total = total + jnp.sum(e.reshape(kb // 8, 8, shard), axis=0)
        total = jnp.sum(total, axis=0, keepdims=True)
        p = peak * SHARP
        l = p + jnp.log(total)
        for t in range(wide):
            peak_ref[pl.ds(block * wide + t, 1), :] = p[:, t * LANES : (t + 1) * LANES]
            lse[pl.ds(block * wide + t, 1), :] = l[:, t * LANES : (t + 1) * LANES]

    def pair(i, peak0):
        block = 2 * i
        peak1 = score(block + 1, 1)
        exponents(block, 0, peak0)
        peak0 = score(jnp.minimum(block + 2, rows - 1), 0)
        exponents(block + 1, 1, peak1)
        return peak0

    lax.fori_loop(0, rows // 2, pair, score(0, 0))
    nt = rows * wide
    copies = send_ref.shape[0]
    send_ref[:, :nt, :] = jnp.broadcast_to(lse[...][None], (copies, nt, LANES))
    for t in range(wide):
        send_ref[:, nt + t : nt + t + 1, :] = jnp.broadcast_to(w_ref[:, t * LANES : (t + 1) * LANES][None], (copies, 1, LANES))


def row_factor(first, got_ref, peak_ref, w_ref, factor_ref, nt):
    if first:
        got = got_ref[:, :nt, :]
        top = jnp.max(got, axis=0)
        common = top + jnp.log(jnp.sum(jnp.exp(got - top[None]), axis=0))
        factor = jnp.exp(peak_ref[...] - common)
        return w_ref[...] * factor, factor
    total = jnp.sum(got_ref[...].astype(jnp.float32), axis=0)
    factor = factor_ref[...]
    return w_ref[...] / total * factor, factor


def put_rows(lhs, r, n):
    hi, lo = split2(r)
    for t in range(n // LANES):
        lhs[0:8, t * LANES : (t + 1) * LANES] = jnp.broadcast_to(r[t : t + 1, :], (8, LANES)).astype(jnp.bfloat16)
        lhs[8:16, t * LANES : (t + 1) * LANES] = jnp.broadcast_to(
            r[t : t + 1, :] - hi[t : t + 1, :].astype(jnp.float32), (8, LANES)
        ).astype(jnp.bfloat16)


def iterate_body(*refs, first, balance, code, kb):
    if first:
        got_ref, peak_ref, w_in, x_ref, col_ref, send_ref, factor_ref, w_ref, lhs = refs
        nt = peak_ref.shape[0]
        if w_in is None or got_ref.shape[0] > 1:
            wt = got_ref.shape[1] - nt
            for b in range(nt // wt):
                w_ref[b * wt : (b + 1) * wt, :] = got_ref[b * code, nt:, :]
        else:
            w_ref[...] = w_in[...]
    else:
        got_ref, factor_ref, w_ref, x_ref, col_ref, send_ref, lhs = refs
        peak_ref = None
    nt = factor_ref.shape[0]
    n = nt * LANES
    kl = x_ref.shape[0]
    r, factor = row_factor(first, got_ref, peak_ref, w_ref, factor_ref, nt)
    if first:
        factor_ref[...] = factor
    put_rows(lhs, r, n)
    acc = jnp.zeros((16, n), jnp.float32)
    for k in range(0, kl, kb):
        x = x_ref[k : k + kb, :]
        cols = lax.dot_general(lhs[...], x, NT, preferred_element_type=jnp.float32)
        col = balance / (cols[0:1] + cols[8:9])
        col_ref[:, k : k + kb] = col
        hi, lo = split2(jnp.broadcast_to(col, (8, kb)))
        acc = acc + lax.dot_general(jnp.concatenate([hi, lo], axis=0), x, NN, preferred_element_type=jnp.float32)
    sums = acc[0:1] + acc[8:9]
    for t in range(nt):
        part = sums[:, t * LANES : (t + 1) * LANES] * factor[t : t + 1, :]
        send_ref[:, t : t + 1, :] = jnp.broadcast_to(part.astype(jnp.bfloat16)[None], (send_ref.shape[0], 1, LANES))


def final_body(me_ref, got_ref, factor_ref, w_ref, x_ref, col_ref, pieces_ref, book_ref, grad_ref, load_ref, lhs, weighted, rt, stage, sems, *, size, code, rows, balance, kb):
    nt = w_ref.shape[0]
    n = nt * LANES
    r, _ = row_factor(False, got_ref, None, w_ref, factor_ref, nt)
    put_rows(lhs, r, n)
    wide = nt // rows
    rt[...] = r.reshape(rows, wide, LANES)

    def weigh(b, _):
        block = load_block(me_ref, pieces_ref, b, size, code)
        cols = jnp.concatenate([rt[b], jnp.zeros((8 - wide % 8, LANES), jnp.float32)], axis=0).T
        for t in range(wide):
            scaled = block[t * LANES : (t + 1) * LANES, :].astype(jnp.float32) * cols[:, t : t + 1]
            weighted[pl.ds(pl.multiple_of((b * wide + t) * LANES, LANES), LANES), :] = scaled.astype(jnp.bfloat16)
        return 0

    lax.fori_loop(0, rows, weigh, 0, unroll=min(rows, 4))
    kl = x_ref.shape[0]
    copies = []
    for i, k in enumerate(range(0, kl, kb)):
        x = x_ref[k : k + kb, :]
        cols = lax.dot_general(lhs[...], x, NT, preferred_element_type=jnp.float32)
        col = col_ref[:, k : k + kb]
        mass = col * (cols[0:1] + cols[8:9]) / balance
        load_ref[:, k : k + kb] = mass
        both = jnp.concatenate([mass, col / balance, jnp.zeros((6, kb), jnp.float32)], axis=0).T
        sums = jnp.dot(x, weighted[...], preferred_element_type=jnp.float32)
        stage[k : k + kb, :] = both[:, 0:1] * book_ref[k : k + kb, :].astype(jnp.float32) - both[:, 1:2] * sums
        copy = pltpu.make_async_copy(stage.at[k : k + kb, :], grad_ref.at[k : k + kb, :], sems.at[i])
        copy.start()
        copies.append(copy)
    for copy in copies:
        copy.wait()


def share_first(send, weights, nt):
    if send.shape[0] == 1:
        lse = send[0, :nt, :]
        top = lax.pmax(lse, AXES)
        common = top + jnp.log(lax.psum(jnp.exp(lse - top), AXES))
        return common[None], lax.all_gather(weights, "rows", axis=0, tiled=True).reshape(nt, LANES)
    got = lax.all_to_all(send, AXES, split_axis=0, concat_axis=0, tiled=True)
    return got, jnp.zeros((8, LANES), jnp.float32)


def share(send):
    if send.shape[0] == 1:
        return lax.psum(send.astype(jnp.float32), AXES)
    return lax.all_to_all(send, AXES, split_axis=0, concat_axis=0, tiled=True)


def copies_of(size, nt):
    return size if size * nt * LANES <= 1 << 20 else 1


IN_VMEM = pl.BlockSpec(memory_space=pltpu.VMEM)
IN_SMEM = pl.BlockSpec(memory_space=pltpu.SMEM)


def call(body, name, args, outs, scratch, out_specs=None):
    return pl.pallas_call(
        body,
        in_specs=[IN_SMEM if a.dtype == jnp.int32 else IN_VMEM for a in args],
        out_specs=out_specs or [IN_VMEM] * len(outs),
        out_shape=outs,
        scratch_shapes=scratch,
        compiler_params=pltpu.CompilerParams(vmem_limit_bytes=VMEM_LIMIT),
        name=name,
    )(*args)


def local(embedding_vectors, codebook, weights):
    rows, code = lax.axis_size("rows"), lax.axis_size("code")
    size = rows * code
    shard, d = embedding_vectors.shape
    kl = codebook.shape[0]
    n = rows * shard
    nt = n // LANES
    wt = shard // LANES
    balance = n / (size * kl)
    copies = copies_of(size, nt)
    me = (lax.axis_index("rows") * code + lax.axis_index("code")).astype(jnp.int32).reshape(1)
    per = shard // code
    piece = lax.dynamic_slice_in_dim(embedding_vectors, lax.axis_index("code") * per, per, 0)
    pieces = gather_pieces(piece, size)
    vec = jax.ShapeDtypeStruct((nt, LANES), jnp.float32)
    lhs = pltpu.VMEM((16, n), jnp.bfloat16)
    kb = min(512, kl)
    x, peak, send = call(
        functools.partial(exponent_body, size=size, code=code, rows=rows, kb=min(256, kl)),
        "exponents",
        (me, pieces, codebook, weights.reshape(1, shard)),
        [pltpu.VMEM((kl, n), jnp.bfloat16), vec, jax.ShapeDtypeStruct((copies, nt + wt, LANES), jnp.float32)],
        [pltpu.VMEM((2, kl, shard), jnp.float32), pltpu.VMEM((nt, LANES), jnp.float32)],
    )
    x = pltpu.with_memory_space_constraint(x, pltpu.VMEM)
    got, w = share_first(send, weights, nt)
    messages = jax.ShapeDtypeStruct((copies, nt, LANES), jnp.bfloat16)
    columns = jax.ShapeDtypeStruct((1, kl), jnp.float32)
    body = functools.partial(iterate_body, balance=balance, code=code, kb=kb)
    col, send, factor, w = call(functools.partial(body, first=True), "iterate_first", (got, peak, w, x), [columns, messages, vec, vec], [lhs])
    got = share(send)
    for _ in range(ITERS - 1):
        col, send = call(functools.partial(body, first=False), "iterate", (got, factor, w, x), [columns, messages], [lhs])
        got = share(send)
    steps = kl // kb
    grad, load = call(
        functools.partial(final_body, size=size, code=code, rows=rows, balance=balance, kb=kb),
        "finish",
        (me, got, factor, w, x, col, pieces, codebook),
        [jax.ShapeDtypeStruct((kl, d), jnp.float32), columns],
        [
            lhs,
            pltpu.VMEM((n, d), jnp.bfloat16),
            pltpu.VMEM((rows, wt, LANES), jnp.float32),
            pltpu.VMEM((kl, d), jnp.float32),
            pltpu.SemaphoreType.DMA((steps,)),
        ],
        [pl.BlockSpec(memory_space=pl.ANY), IN_VMEM],
    )
    return grad, load.reshape(kl)


def solution(mesh):
    placed = (P("rows", None), P(("code", "rows"), None), P("rows"))
    return jax.shard_map(
        local,
        mesh=mesh,
        in_specs=placed,
        out_specs=(P(("code", "rows"), None), P(("code", "rows"))),
        check_vma=False,
    )
```

time: 935 us -> 116 us (0.12)
  waiting for transfers between devices: 665 us -> 12.4 us
  matrix products: 191 us -> 0 us
  Pallas kernels: 0 us -> 35.2 us
  other arithmetic: 19.1 us -> 0.03 us
  blocking collectives: 35.5 us -> 53.2 us
  between operations: 15.3 us -> 0.87 us
    reduce_scatter x1 -> x0, waiting for transfers between devices: 287 us -> none  [local(): lax.psum_scatter(partial_aggregates, 'rows', scatter_dimension=0, tiled=T...]
    psum x3 -> x0, waiting for transfers between devices: 199 us -> none  [local(): col_scale = balance / lax.psum(partial_cols, 'rows')]
    dot_general x9 -> x0, matrix products: 191 us -> none  [the longest x4 105 us: marginal_per_sample(): jnp.dot(power_term, col_scale, precision=lax.Precision.HIGHEST)]
    all_gather x1 -> x0, waiting for transfers between devices: 129 us -> none  [local(): lax.all_gather(codebook, 'rows', axis=0, tiled=True)]
    all_to_all x0 -> x4, blocking collectives: none -> 53.2 us  [the longest x3 35.3 us: share(): return lax.all_to_all(send, AXES, split_axis=0, concat_axis=0, tiled=True)]
    unnamed x7 -> x0, waiting for transfers between devices: 51.2 us -> none
    pallas_call x0 -> x5, Pallas kernels: none -> 35.2 us  [call(): pl.pallas_call(body, in_specs=[IN_SMEM if a.dtype == jnp.int32 else IN_VM...]
    psum x4 -> x0, blocking collectives: 29.4 us -> none  [marginal_per_sample(): lax.psum(jnp.dot(power_term, col_scale, precision=lax.Precision.HIGHEST),...]
  transfers between devices with their start and end apart: 6 -> 7, of which waited for: 6 -> 5; matrix products, arithmetic and copies ran while one was open for 2% -> 3% of each run, Pallas kernels for 0% -> 0%
where the time goes in v2:
time: 116 us
  blocking collectives  53.2 us (46%)
  Pallas kernels  35.2 us (30%)
  waiting for transfers between devices  12.4 us (11%)
  starting transfers between devices  8.99 us (8%)
  local copies, waits for them, and re-layouts  5.48 us (5%)
    all_to_all x3, blocking collectives, share(): return lax.all_to_all(send, AXES, split_axis=0, concat_axis=0, tiled=True)  35.3 us
    pallas_call x5, Pallas kernels, call(): pl.pallas_call(body, in_specs=[IN_SMEM if a.dtype == jnp.int32 else IN_VM...  35.2 us
    all_to_all x1, blocking collectives, share_first(): got = lax.all_to_all(send, AXES, split_axis=0, concat_axis=0, tiled=True)  18 us
    ppermute x7, waiting for transfers between devices, exchange(): return lax.ppermute(x, AXES, [(i, i ^ mask) for i in range(size)])  12.4 us
    ppermute x7, starting transfers between devices, exchange(): return lax.ppermute(x, AXES, [(i, i ^ mask) for i in range(size)])  8.99 us
    unnamed x11, local copies, waits for them, and re-layouts  4.73 us
  transfers between devices with their start and end apart: 7, of which 5 were waited for; matrix products, arithmetic and copies ran while one was open for 3% of the time, Pallas kernels for 0%

profile of v2, /device:TPU:1, one launch (start us, length us, event | category | flops | bytes accessed | tf_op | source)
XLA Modules:
  0.0 116.2 jit_solution(2384130109708227458)
XLA Ops:
  0.6 0.0 copy-start.1
  0.6 1.4 %constant_dynamic-update-slice_fusion.6 = (bf16[16,96,256]{2,1,0:T(8,128)(2,1)}, bf16[1,96,256]{2,1,0:T(8,128)(2,1)S(1)}) fusion(bf16[384,256]{1,0:T(8,128)(2,1)} %param.3, s32[]{:T(128)S(6)} %select_n.3), kind=kLoop, calls=%fused_computation.8 | loop fusion | bytes 147460
  2.1 4.2 %collective-permute-start.2 = (bf16[1,96,256]{2,1,0:T(8,128)(2,1)S(1)}, bf16[1,96,256]{2,1,0:T(8,128)(2,1)S(1)}, u32[]{:S(2)}, u32[]{:S(2)}) collective-permute-start(bf16[1,96,256]{2,1,0:T(8,128)(2,1)S(1)} %get-tuple-element.25), channel_id=1, source_target_pairs={{0,24},{1,25},{2,26},{3,27},{4,28},{5,29},{6,30},{7,31},{8,16},{9,... | collective-permute-start | bytes 147464 | tf_op jit(solution)/shard_map/ppermute | solution.py:26
  6.2 0.0 collective-permute-start.1
  6.2 0.3 collective-permute-start
  6.5 1.2 %collective-permute-done.2 = bf16[1,96,256]{2,1,0:T(8,128)(2,1)S(1)} collective-permute-done((bf16[1,96,256]{2,1,0:T(8,128)(2,1)S(1)}, bf16[1,96,256]{2,1,0:T(8,128)(2,1)S(1)}, u32[]{:S(2)}, u32[]{:S(2)}) %collective-permute-start.2) | collective-permute-done | bytes 49184 | tf_op jit(solution)/shard_map/ppermute | solution.py:26
  7.7 2.9 %collective-permute-done.1 = bf16[1,96,256]{2,1,0:T(8,128)(2,1)S(1)} collective-permute-done((bf16[1,96,256]{2,1,0:T(8,128)(2,1)S(1)}, bf16[1,96,256]{2,1,0:T(8,128)(2,1)S(1)}, u32[]{:S(2)}, u32[]{:S(2)}) %collective-permute-start.1) | collective-permute-done | bytes 49184 | tf_op jit(solution)/shard_map/ppermute | solution.py:26
  10.6 0.0 collective-permute-done
  10.6 2.2 %collective-permute-start.5 = (bf16[4,96,256]{2,1,0:T(8,128)(2,1)S(1)}, bf16[4,96,256]{2,1,0:T(8,128)(2,1)S(1)}, u32[]{:S(2)}, u32[]{:S(2)}) collective-permute-start(bf16[4,96,256]{2,1,0:T(8,128)(2,1)S(1)} %pad_maximum_fusion), channel_id=1, source_target_pairs={{0,6},{1,7},{2,4},{3,5},{4,2},{5,3},{6,0},{7,1},{8,14},{9,15},{10,... | collective-permute-start | bytes 589832 | tf_op jit(solution)/shard_map/ppermute | solution.py:26
  12.9 0.2 collective-permute-start.4
  13.1 0.3 collective-permute-start.3
  13.4 0.6 constant_dynamic-update-slice_fusion.5
  14.0 0.6 constant_dynamic-update-slice_fusion.4
  14.6 0.6 constant_dynamic-update-slice_fusion.3
  15.2 5.5 %collective-permute-done.3 = bf16[4,96,256]{2,1,0:T(8,128)(2,1)S(1)} collective-permute-done((bf16[4,96,256]{2,1,0:T(8,128)(2,1)S(1)}, bf16[4,96,256]{2,1,0:T(8,128)(2,1)S(1)}, u32[]{:S(2)}, u32[]{:S(2)}) %collective-permute-start.3) | collective-permute-done | bytes 196640 | tf_op jit(solution)/shard_map/ppermute | solution.py:26
  20.8 0.0 copy-start
  20.8 0.7 constant_dynamic-update-slice_fusion.2
  21.5 0.6 collective-permute-done.4
  22.1 0.7 constant_dynamic-update-slice_fusion.1
  22.8 0.0 collective-permute-done.5
  22.8 0.7 constant_dynamic-update-slice_fusion
  23.5 1.8 %collective-permute-start.6 = (bf16[16,96,256]{2,1,0:T(8,128)(2,1)}, bf16[16,96,256]{2,1,0:T(8,128)(2,1)S(1)}, u32[]{:S(2)}, u32[]{:S(2)}) collective-permute-start(bf16[16,96,256]{2,1,0:T(8,128)(2,1)} %get-tuple-element.26), channel_id=1, source_target_pairs={{0,1},{1,0},{2,3},{3,2},{4,5},{5,4},{6,7},{7,6},{8,9},{9,8},{10,11... | collective-permute-start | bytes 2359304 | tf_op jit(solution)/shard_map/ppermute | solution.py:26
  25.4 0.0 copy-done.1
  25.4 2.1 %collective-permute-done.6 = bf16[16,96,256]{2,1,0:T(8,128)(2,1)S(1)} collective-permute-done((bf16[16,96,256]{2,1,0:T(8,128)(2,1)}, bf16[16,96,256]{2,1,0:T(8,128)(2,1)S(1)}, u32[]{:S(2)}, u32[]{:S(2)}) %collective-permute-start.6) | collective-permute-done | bytes 786464 | tf_op jit(solution)/shard_map/ppermute | solution.py:26
  27.5 0.1 constant_dynamic-update-slice_fusion.7.pieces_ref
  27.5 0.0 copy-done
  27.5 9.4 %exponents.1 = (bf16[2048,3072]{1,0:T(8,128)(2,1)S(1)}, f32[24,128]{1,0:T(8,128)S(1)}, f32[32,27,128]{2,1,0:T(8,128)S(1)}) custom-call(s32[1]{0:T(128)} %bitcast.me_ref, bf16[32,96,256]{2,1,0:T(8,128)(2,1)S(1)} %constant_dynamic-update-slice_fusion.7.pieces_ref, bf16[2048,256]{1,0:T(8,128)(2,1)S(1)} %copy-done, f32[1,384]{1,0:T(1,128)S(1)} %reshape.14.w_ref), custom_call_target="tpu_custom_call" | custom-call | tf_op jit(solution)/shard_map/exponents/pallas_call | solution.py:220
  36.9 18.0 %all_to_all.20.refs_0_ = f32[32,27,128]{2,1,0:T(8,128)S(1)} all-to-all(f32[32,27,128]{2,1,0:T(8,128)S(1)} %get-tuple-element.13), channel_id=1, replica_groups=mesh['rows'=8,'code'=4] {'rows','code'}, dimensions={0} | all-to-all | bytes 884736 | tf_op jit(solution)/shard_map/all_to_all | solution.py:201
  54.9 5.5 %iterate_first.1 = (f32[1,2048]{1,0:T(1,128)}, bf16[32,24,128]{2,1,0:T(8,128)(2,1)S(1)}, f32[24,128]{1,0:T(8,128)S(1)}, f32[24,128]{1,0:T(8,128)S(1)}) custom-call(f32[32,27,128]{2,1,0:T(8,128)S(1)} %all_to_all.20.refs_0_, f32[24,128]{1,0:T(8,128)S(1)} %get-tuple-element.14.refs_1_, f32[8,128]{1,0:T(8,128)S(1)} %broadcast_in_dim.7.refs_2_, ...), custom_call_target="tpu_custom_call" | custom-call | tf_op jit(solution)/shard_map/iterate_first/pallas_call | solution.py:220
  60.4 12.5 %all_to_all.21.refs_0_ = bf16[32,24,128]{2,1,0:T(8,128)(2,1)S(1)} all-to-all(bf16[32,24,128]{2,1,0:T(8,128)(2,1)S(1)} %get-tuple-element.16), channel_id=1, replica_groups=mesh['rows'=8,'code'=4] {'rows','code'}, dimensions={0} | all-to-all | bytes 393216 | tf_op jit(solution)/shard_map/all_to_all | solution.py:208
  72.9 5.4 %iterate.2 = (f32[1,2048]{1,0:T(1,128)}, bf16[32,24,128]{2,1,0:T(8,128)(2,1)S(1)}) custom-call(bf16[32,24,128]{2,1,0:T(8,128)(2,1)S(1)} %all_to_all.21.refs_0_, f32[24,128]{1,0:T(8,128)S(1)} %get-tuple-element.17.refs_1_.factor_ref, f32[24,128]{1,0:T(8,128)S(1)} %get-tuple-element.18.refs_2_.w_ref, bf16[2048,3072]{1,0:T(8,128)(2,1)S(1)} %get-tuple-element.15.refs_3_.x_ref), custom_call_target="tpu_custom_call" | custom-call | tf_op jit(solution)/shard_map/iterate/pallas_call | solution.py:220
  78.3 11.4 %all_to_all.22.refs_0_ = bf16[32,24,128]{2,1,0:T(8,128)(2,1)S(1)} all-to-all(bf16[32,24,128]{2,1,0:T(8,128)(2,1)S(1)} %get-tuple-element.19), channel_id=1, replica_groups=mesh['rows'=8,'code'=4] {'rows','code'}, dimensions={0} | all-to-all | bytes 393216 | tf_op jit(solution)/shard_map/all_to_all | solution.py:208
  89.7 5.4 %iterate.3 = (f32[1,2048]{1,0:T(1,128)S(1)}, bf16[32,24,128]{2,1,0:T(8,128)(2,1)S(1)}) custom-call(bf16[32,24,128]{2,1,0:T(8,128)(2,1)S(1)} %all_to_all.22.refs_0_, f32[24,128]{1,0:T(8,128)S(1)} %get-tuple-element.17.refs_1_.factor_ref, f32[24,128]{1,0:T(8,128)S(1)} %get-tuple-element.18.refs_2_.w_ref, bf16[2048,3072]{1,0:T(8,128)(2,1)S(1)} %get-tuple-element.15.refs_3_.x_ref), custom_call_target="tpu_custom_call" | custom-call | tf_op jit(solution)/shard_map/iterate/pallas_call | solution.py:220
  95.1 11.4 %all_to_all.23.got_ref = bf16[32,24,128]{2,1,0:T(8,128)(2,1)S(1)} all-to-all(bf16[32,24,128]{2,1,0:T(8,128)(2,1)S(1)} %get-tuple-element.20), channel_id=1, replica_groups=mesh['rows'=8,'code'=4] {'rows','code'}, dimensions={0} | all-to-all | bytes 393216 | tf_op jit(solution)/shard_map/all_to_all | solution.py:208
  106.6 9.5 %finish.1 = (f32[2048,256]{1,0:T(8,128)}, f32[1,2048]{1,0:T(1,128)}) custom-call(s32[1]{0:T(128)} %bitcast.me_ref, bf16[32,24,128]{2,1,0:T(8,128)(2,1)S(1)} %all_to_all.23.got_ref, f32[24,128]{1,0:T(8,128)S(1)} %get-tuple-element.17.refs_1_.factor_ref, f32[24,128]{1,0:T(8,128)S(1)} %get-tuple-element.18.refs_2_.w_ref, ...), custom_call_target="tpu_custom_call" | custom-call | tf_op jit(solution)/shard_map/finish/pallas_call | solution.py:220
  (4 shorter events, 0.0 us)
Async XLA Ops:
  0.6 24.7 %copy-start.1 = (f32[384]{0:T(512)S(1)}, f32[384]{0:T(512)}, u32[]{:S(2)}) copy-start(f32[384]{0:T(512)} %param.5) | copy-start | bytes 4612
  2.1 5.7 %collective-permute-start.2 = (bf16[1,96,256]{2,1,0:T(8,128)(2,1)S(1)}, bf16[1,96,256]{2,1,0:T(8,128)(2,1)S(1)}, u32[]{:S(2)}, u32[]{:S(2)}) collective-permute-start(bf16[1,96,256]{2,1,0:T(8,128)(2,1)S(1)} %get-tuple-element.25), channel_id=1, source_target_pairs={{0,24},{1,25},{2,26},{3,27},{4,28},{5,29},{6,30},{7,31},{8,16},{9,... | collective-permute-start | bytes 147464 | tf_op jit(solution)/shard_map/ppermute | solution.py:26
  6.2 4.4 %collective-permute-start.1 = (bf16[1,96,256]{2,1,0:T(8,128)(2,1)S(1)}, bf16[1,96,256]{2,1,0:T(8,128)(2,1)S(1)}, u32[]{:S(2)}, u32[]{:S(2)}) collective-permute-start(bf16[1,96,256]{2,1,0:T(8,128)(2,1)S(1)} %get-tuple-element.25), channel_id=1, source_target_pairs={{0,16},{1,17},{2,18},{3,19},{4,20},{5,21},{6,22},{7,23},{8,24},{9,... | collective-permute-start | bytes 147464 | tf_op jit(solution)/shard_map/ppermute | solution.py:26
  6.2 4.4 %collective-permute-start = (bf16[1,96,256]{2,1,0:T(8,128)(2,1)S(1)}, bf16[1,96,256]{2,1,0:T(8,128)(2,1)S(1)}, u32[]{:S(2)}, u32[]{:S(2)}) collective-permute-start(bf16[1,96,256]{2,1,0:T(8,128)(2,1)S(1)} %get-tuple-element.25), channel_id=1, source_target_pairs={{0,8},{1,9},{2,10},{3,11},{4,12},{5,13},{6,14},{7,15},{8,0},{9,1},... | collective-permute-start | bytes 147464 | tf_op jit(solution)/shard_map/ppermute | solution.py:26
  10.6 12.2 %collective-permute-start.5 = (bf16[4,96,256]{2,1,0:T(8,128)(2,1)S(1)}, bf16[4,96,256]{2,1,0:T(8,128)(2,1)S(1)}, u32[]{:S(2)}, u32[]{:S(2)}) collective-permute-start(bf16[4,96,256]{2,1,0:T(8,128)(2,1)S(1)} %pad_maximum_fusion), channel_id=1, source_target_pairs={{0,6},{1,7},{2,4},{3,5},{4,2},{5,3},{6,0},{7,1},{8,14},{9,15},{10,... | collective-permute-start | bytes 589832 | tf_op jit(solution)/shard_map/ppermute | solution.py:26
  12.9 9.2 %collective-permute-start.4 = (bf16[4,96,256]{2,1,0:T(8,128)(2,1)S(1)}, bf16[4,96,256]{2,1,0:T(8,128)(2,1)S(1)}, u32[]{:S(2)}, u32[]{:S(2)}) collective-permute-start(bf16[4,96,256]{2,1,0:T(8,128)(2,1)S(1)} %pad_maximum_fusion), channel_id=1, source_target_pairs={{0,4},{1,5},{2,6},{3,7},{4,0},{5,1},{6,2},{7,3},{8,12},{9,13},{10,... | collective-permute-start | bytes 589832 | tf_op jit(solution)/shard_map/ppermute | solution.py:26
  13.1 7.7 %collective-permute-start.3 = (bf16[4,96,256]{2,1,0:T(8,128)(2,1)S(1)}, bf16[4,96,256]{2,1,0:T(8,128)(2,1)S(1)}, u32[]{:S(2)}, u32[]{:S(2)}) collective-permute-start(bf16[4,96,256]{2,1,0:T(8,128)(2,1)S(1)} %pad_maximum_fusion), channel_id=1, source_target_pairs={{0,2},{1,3},{2,0},{3,1},{4,6},{5,7},{6,4},{7,5},{8,10},{9,11},{10,... | collective-permute-start | bytes 589832 | tf_op jit(solution)/shard_map/ppermute | solution.py:26
  20.8 6.8 %copy-start = (bf16[2048,256]{1,0:T(8,128)(2,1)S(1)}, bf16[2048,256]{1,0:T(8,128)(2,1)}, u32[]{:S(2)}) copy-start(bf16[2048,256]{1,0:T(8,128)(2,1)} %book_ref.3) | copy-start | bytes 3145732
  23.5 4.0 %collective-permute-start.6 = (bf16[16,96,256]{2,1,0:T(8,128)(2,1)}, bf16[16,96,256]{2,1,0:T(8,128)(2,1)S(1)}, u32[]{:S(2)}, u32[]{:S(2)}) collective-permute-start(bf16[16,96,256]{2,1,0:T(8,128)(2,1)} %get-tuple-element.26), channel_id=1, source_target_pairs={{0,1},{1,0},{2,3},{3,2},{4,5},{5,4},{6,7},{7,6},{8,9},{9,8},{10,11... | collective-permute-start | bytes 2359304 | tf_op jit(solution)/shard_map/ppermute | solution.py:26

commit v3 on v2

v3 whole, which is shorter than its diff:
```python
import functools

import jax
import jax.numpy as jnp
import numpy as np
from jax import lax
from jax.experimental import pallas as pl
from jax.experimental.pallas import tpu as pltpu
from jax.sharding import PartitionSpec as P

ITERS = 3
SHARP = 2.0
LOG2E = 1.4426950408889634
AXES = ("rows", "code")
MANY = 64
LANES = 128
VMEM_LIMIT = 32 * 1024 * 1024
NT = (((1,), (1,)), ((), ()))
NN = (((1,), (0,)), ((), ()))


def bit_groups(size):
    bits = [1 << b for b in range(size.bit_length() - 1)][::-1]
    return [tuple(bits[i : i + 2]) for i in range(0, len(bits), 2)]


def exchange(x, mask, size):
    return lax.ppermute(x, AXES, [(i, i ^ mask) for i in range(size)])


def gather_blocks(piece, size):
    groups = bit_groups(size)
    segments = None
    for i, group in enumerate(groups):
        masks = group if len(group) == 1 else (group[1], group[0], group[0] ^ group[1])
        if segments is None:
            first = piece[None]
            segments = [jnp.concatenate([first] + [exchange(first, m, size) for m in masks], axis=0)[None]]
        else:
            if size > MANY:
                segments = [jnp.concatenate(segments, axis=0)]
            segments = segments + [exchange(x, m, size) for m in masks for x in segments]
    return segments if size <= MANY else [jnp.concatenate(segments, axis=0)]


def slot_of(device, size):
    slot, place = 0, 1
    for group in bit_groups(size):
        for bit in group[::-1]:
            slot = slot + jnp.where((device & bit) != 0, place, 0)
            place *= 2
    return slot


def split2(x):
    hi = x.astype(jnp.bfloat16)
    lo = (x - hi.astype(jnp.float32)).astype(jnp.bfloat16)
    return hi, lo


def load_block(segments, block, mine):
    count = segments[0].shape[0]
    ref, at = (segments[block], 0) if count == 1 else (segments[0], block)
    return jnp.concatenate([ref[at, j ^ mine] for j in range(ref.shape[1])], axis=0)


def exponent_body(*refs, size, code, first, start, through, kb):
    n_in = len(refs) - 4 - through - (0 if first else 3)
    me_ref, w_ref, book_ref, segments = refs[0], refs[1], refs[2], refs[3:n_in]
    x_ref, peak_ref, lse_ref = refs[len(refs) - 4 - through : len(refs) - 1 - through]
    scores = refs[-1]
    fan, per = segments[0].shape[1:3]
    shard = fan * per
    wide = shard // LANES
    kl = book_ref.shape[0]
    scale = SHARP * LOG2E
    slot = slot_of(me_ref[0], size)
    mine, home = slot & (fan - 1), slot // fan
    count = max(len(segments), segments[0].shape[0])
    if first and fan == code:
        lane = lax.broadcasted_iota(jnp.int32, (8, shard), 1) // per
        moved = pltpu.roll(jnp.broadcast_to(w_ref[...].reshape(1, shard), (8, shard)), ((mine - (me_ref[0] & (code - 1))) & (code - 1)) * per, 1)
        moved = jnp.where(lane == mine, moved, 0.0)
        for t in range(wide):
            lse_ref[lse_ref.shape[0] - wide + t : lse_ref.shape[0] - wide + t + 1, :] = moved[0:1, t * LANES : (t + 1) * LANES]

    def score(block, at):
        e = load_block(segments, block, mine)
        peak = jnp.full((8, shard), -jnp.inf, jnp.float32)
        for k in range(0, kl, kb):
            s = lax.dot_general(book_ref[k : k + kb, :], e, NT, preferred_element_type=jnp.float32)
            scores[at, k : k + kb, :] = s
            peak = jnp.maximum(peak, jnp.max(s.reshape(kb // 8, 8, shard), axis=0))
        return jnp.max(peak, axis=0, keepdims=True)

    def exponents(block, at, peak):
        block = (start[block] if isinstance(block, int) else block) ^ home
        total = jnp.zeros((8, shard), jnp.float32)
        lanes = pl.ds(pl.multiple_of(block * shard, LANES), shard)
        for k in range(0, kl, kb):
            e = jnp.exp2((scores[at, k : k + kb, :] - peak) * scale)
            x_ref[k : k + kb, lanes] = e.astype(jnp.bfloat16)
            total = total + jnp.sum(e.reshape(kb // 8, 8, shard), axis=0)
        total = jnp.sum(total, axis=0, keepdims=True)
        p = peak * SHARP
        l = p + jnp.log(total)
        for t in range(wide):
            peak_ref[pl.ds(block * wide + t, 1), :] = p[:, t * LANES : (t + 1) * LANES]
            lse_ref[pl.ds(block * wide + t, 1), :] = l[:, t * LANES : (t + 1) * LANES]

    if len(segments) == count:
        peak = score(0, 0)
        for i in range(count):
            following = score(i + 1, (i + 1) % 2) if i + 1 < count else None
            exponents(i, i % 2, peak)
            peak = following
        return

    def pair(i, peak0):
        peak1 = score(2 * i + 1, 1)
        exponents(2 * i, 0, peak0)
        peak0 = score(jnp.minimum(2 * i + 2, count - 1), 0)
        exponents(2 * i + 1, 1, peak1)
        return peak0

    lax.fori_loop(0, count // 2, pair, score(0, 0))


def row_factor(first, got_ref, peak_ref, w_ref, factor_ref, nt):
    if first:
        got = got_ref[:, :nt, :]
        top = jnp.max(got, axis=0)
        common = top + jnp.log(jnp.sum(jnp.exp(got - top[None]), axis=0))
        factor = jnp.exp(peak_ref[...] - common)
        return w_ref[...] * factor, factor
    total = jnp.sum(got_ref[...].astype(jnp.float32), axis=0)
    factor = factor_ref[...]
    return w_ref[...] / total * factor, factor


def put_rows(dst, r):
    for t in range(r.shape[0]):
        dst[:, t * LANES : (t + 1) * LANES] = jnp.broadcast_to(r[t : t + 1, :], (8, LANES))


def column_sums(x_ref, r_ref, k, kb):
    parts = []
    for g in range(k, k + kb, 16):
        sums = [None, None]
        for t in range(r_ref.shape[1] // LANES):
            lanes = slice(t * LANES, (t + 1) * LANES)
            term = x_ref[g : g + 16, lanes].astype(jnp.float32) * jnp.broadcast_to(r_ref[0:1, lanes], (16, LANES))
            sums[t % 2] = term if sums[t % 2] is None else sums[t % 2] + term
        parts.append(sums[0] + sums[1])
    return jnp.sum(jnp.concatenate(parts, axis=0).T, axis=0, keepdims=True)


def iterate_body(*refs, first, balance, kb, plan):
    if first:
        got_ref, peak_ref, x_ref = refs[:3]
        col_ref, send_ref, factor_ref, w_ref, r_rows, acc = refs[-6:]
        nt = peak_ref.shape[0]
        if plan is None:
            w_ref[...] = refs[3][...]
        else:
            wide = (got_ref.shape[1] - nt) // 2
            for b, sources in enumerate(plan):
                parts = [got_ref[i, nt + wide * c : nt + wide * (c + 1), :] for i, c in sources]
                w_ref[b * wide : (b + 1) * wide, :] = functools.reduce(jnp.add, parts)
    else:
        got_ref, factor_ref, w_ref, x_ref, col_ref, send_ref, r_rows, acc = refs
        peak_ref = None
    nt = factor_ref.shape[0]
    n = nt * LANES
    kl = x_ref.shape[0]
    r, factor = row_factor(first, got_ref, peak_ref, w_ref, factor_ref, nt)
    if first:
        factor_ref[...] = factor
    put_rows(r_rows, r)
    acc[...] = jnp.zeros(acc.shape, jnp.float32)

    def add_rows(k, col):
        hi, lo = split2(jnp.broadcast_to(col, (8, kb)))
        acc[...] += jnp.dot(jnp.concatenate([hi, lo], axis=0), x_ref[k : k + kb, :], preferred_element_type=jnp.float32)

    before = None
    for k in range(0, kl, kb):
        col = balance / column_sums(x_ref, r_rows, k, kb)
        col_ref[:, k : k + kb] = col
        if before is not None:
            add_rows(k - kb, before)
        before = col
    add_rows(kl - kb, before)
    sums = acc[0:1, :] + acc[8:9, :]
    for t in range(nt):
        part = sums[:, t * LANES : (t + 1) * LANES] * factor[t : t + 1, :]
        send_ref[:, t : t + 1, :] = jnp.broadcast_to(part.astype(jnp.bfloat16)[None], (send_ref.shape[0], 1, LANES))


def final_body(*refs, size, balance, kb):
    me_ref, got_ref, factor_ref, w_ref, x_ref, col_ref, book_ref = refs[:7]
    segments = refs[7:-7]
    grad_ref, load_ref, r_rows, weighted, rt, stage, sems = refs[-7:]
    nt = w_ref.shape[0]
    n = nt * LANES
    r, _ = row_factor(False, got_ref, None, w_ref, factor_ref, nt)
    put_rows(r_rows, r)
    fan, per = segments[0].shape[1:3]
    wide = fan * per // LANES
    blocks = nt // wide
    rt[...] = r.reshape(blocks, wide, LANES)
    slot = slot_of(me_ref[0], size)
    mine, home = slot & (fan - 1), slot // fan

    def weigh(i, _):
        block = load_block(segments, i, mine)
        b = i ^ home
        cols = jnp.concatenate([rt[b], jnp.zeros((8 - wide % 8, LANES), jnp.float32)], axis=0).T
        for t in range(wide):
            scaled = block[t * LANES : (t + 1) * LANES, :].astype(jnp.float32) * cols[:, t : t + 1]
            weighted[pl.ds(pl.multiple_of((b * wide + t) * LANES, LANES), LANES), :] = scaled.astype(jnp.bfloat16)
        return 0

    if len(segments) == blocks:
        for i in range(blocks):
            weigh(i, 0)
    else:
        lax.fori_loop(0, blocks, weigh, 0)
    kl = x_ref.shape[0]
    copies = []
    for i, k in enumerate(range(0, kl, kb)):
        x = x_ref[k : k + kb, :]
        col = col_ref[:, k : k + kb]
        mass = col * column_sums(x_ref, r_rows, k, kb) / balance
        load_ref[:, k : k + kb] = mass
        both = jnp.concatenate([mass, col / balance, jnp.zeros((6, kb), jnp.float32)], axis=0).T
        sums = jnp.dot(x, weighted[...], preferred_element_type=jnp.float32)
        stage[k : k + kb, :] = both[:, 0:1] * book_ref[k : k + kb, :].astype(jnp.float32) - both[:, 1:2] * sums
        copy = pltpu.make_async_copy(stage.at[k : k + kb, :], grad_ref.at[k : k + kb, :], sems.at[i])
        copy.start()
        copies.append(copy)
    for copy in copies:
        copy.wait()


def join_body(me_ref, own_ref, other_ref, out_ref, *, nt):
    wide = own_ref.shape[0] - nt
    copies = out_ref.shape[0]
    a, b = own_ref[:nt, :], other_ref[:nt, :]
    top = jnp.maximum(a, b)
    joined = top + jnp.log(jnp.exp(a - top) + jnp.exp(b - top))
    out_ref[:, :nt, :] = jnp.broadcast_to(joined[None], (copies, nt, LANES))
    odd = (me_ref[0] & 1) == 1
    a, b = own_ref[nt:, :], other_ref[nt:, :]
    out_ref[:, nt : nt + wide, :] = jnp.broadcast_to(jnp.where(odd, b, a)[None], (copies, wide, LANES))
    out_ref[:, nt + wide :, :] = jnp.broadcast_to(jnp.where(odd, a, b)[None], (copies, wide, LANES))


def share_first(lse, weights, me1, size, copies, nt):
    shard = weights.shape[0]
    code = lax.axis_size("code")
    groups = bit_groups(size)
    fan = 1 << len(groups[0])
    if copies == 1:
        lse = lse[:nt]
        top = lax.pmax(lse, AXES)
        common = top + jnp.log(lax.psum(jnp.exp(lse - top), AXES))
        w = lax.all_gather(weights, "rows", axis=0, tiled=True).reshape(size, shard // code)
        order = np.argsort([slot_int(g, size) for g in range(size)])
        return common[None], w[order].reshape(nt, LANES), None
    other = exchange(lse, 1, size)
    wide = lse.shape[0] - nt
    (message,) = call(
        functools.partial(join_body, nt=nt),
        "join",
        (me1, lse, other),
        [jax.ShapeDtypeStruct((size // 2, nt + 2 * wide, LANES), jnp.float32)],
        [],
    )
    same = [[i for i in range(size) if i % 2 == c] for c in range(2)]
    got = lax.all_to_all(message, AXES, split_axis=0, concat_axis=0, tiled=True, axis_index_groups=same)
    plan = [[] for _ in range(size // fan)]
    for g in range(size):
        plan[slot_int(g, size) // fan].append((g // 2, g % 2))
    return got, None, plan


def slot_int(device, size):
    bits = [bit for group in bit_groups(size) for bit in group[::-1]]
    return sum(1 << i for i, bit in enumerate(bits) if device & bit)


def share(send):
    if send.shape[0] == 1:
        return lax.psum(send.astype(jnp.float32), AXES)
    return lax.all_to_all(send, AXES, split_axis=0, concat_axis=0, tiled=True)


def copies_of(size, nt):
    return size if size * nt * LANES <= 1 << 20 else 1


IN_VMEM = pl.BlockSpec(memory_space=pltpu.VMEM)
IN_SMEM = pl.BlockSpec(memory_space=pltpu.SMEM)


def call(body, name, args, outs, scratch, out_specs=None, aliases=None, cost=None):
    return pl.pallas_call(
        body,
        in_specs=[IN_SMEM if a.dtype == jnp.int32 else IN_VMEM for a in args],
        out_specs=out_specs or [IN_VMEM] * len(outs),
        out_shape=outs,
        scratch_shapes=scratch,
        input_output_aliases=aliases or {},
        cost_estimate=cost,
        compiler_params=pltpu.CompilerParams(vmem_limit_bytes=VMEM_LIMIT),
        name=name,
    )(*args)


def local(embedding_vectors, codebook, weights):
    rows, code = lax.axis_size("rows"), lax.axis_size("code")
    size = rows * code
    shard, d = embedding_vectors.shape
    kl = codebook.shape[0]
    n = rows * shard
    nt = n // LANES
    balance = n / (size * kl)
    copies = copies_of(size, nt)
    me = (lax.axis_index("rows") * code + lax.axis_index("code")).astype(jnp.int32)
    per = shard // code
    piece = lax.dynamic_slice_in_dim(embedding_vectors, lax.axis_index("code") * per, per, 0)
    me1 = me.reshape(1)
    vec = jax.ShapeDtypeStruct((nt, LANES), jnp.float32)
    outs = [pltpu.VMEM((kl, n), jnp.bfloat16), pltpu.VMEM((nt, LANES), jnp.float32)]
    outs.append(pltpu.VMEM((nt + shard // LANES, LANES), jnp.float32))
    block = per << len(bit_groups(size)[0])

    def exponents(state, chosen, part, through=0):
        state = tuple(pltpu.with_memory_space_constraint(a, pltpu.VMEM) for a in state)
        args = (me1, weights, book, *part) + state
        count = sum(p.shape[0] for p in part)
        aliases = {3 + i: 3 + i for i in range(through)}
        if state:
            aliases.update({len(args) - 3 + i: i for i in range(3)})
        out = call(
            functools.partial(exponent_body, size=size, code=code, first=not state, start=chosen, through=through, kb=min(256, kl)),
            "exponents",
            args,
            outs + [jax.ShapeDtypeStruct(p.shape, p.dtype) for p in part[:through]],
            [pltpu.VMEM((2, kl, block), jnp.float32)],
            cost=pl.CostEstimate(
                flops=2 * kl * d * block * count, transcendentals=kl * block * count, bytes_accessed=6 * kl * block * count
            ),
            aliases=aliases,
        )
        return tuple(out[:3]), out[3:]

    book = pltpu.with_memory_space_constraint(codebook, pltpu.VMEM)
    if size == 32:
        first = piece[None]
        a0 = jnp.concatenate([first] + [exchange(first, m, size) for m in (8, 16, 24)], axis=0)[None]
        a1 = exchange(a0, 1, size)
        x0, y0, d0 = (exchange(a0, m, size) for m in (2, 4, 6))
        state, _ = exponents((), [0, 4], [a0, a1])
        state, (x0, y0) = exponents(state, [1, 2], [x0, y0], 2)
        x1, y1 = exchange(x0, 1, size), exchange(y0, 1, size)
        state, (d0,) = exponents(state, [3], [d0], 1)
        d1 = exchange(d0, 1, size)
        state, _ = exponents(state, [5, 6], [x1, y1])
        state, _ = exponents(state, [7], [d1])
        segments = [a0, x0, y0, d0, a1, x1, y1, d1]
    else:
        segments = gather_blocks(piece, size)
        state, _ = exponents((), list(range(len(segments))), segments)
    x, peak, lse = state
    x = pltpu.with_memory_space_constraint(x, pltpu.VMEM)
    got, w, plan = share_first(lse, weights, me1, size, copies, nt)
    rows_f32 = pltpu.VMEM((8, n), jnp.float32)
    kb = min(256, kl)
    scratch = [rows_f32, pltpu.VMEM((16, n), jnp.float32)]
    messages = jax.ShapeDtypeStruct((copies, nt, LANES), jnp.bfloat16)
    columns = jax.ShapeDtypeStruct((1, kl), jnp.float32)
    body = functools.partial(iterate_body, balance=balance, kb=kb, plan=plan)
    col, send, factor, w = call(functools.partial(body, first=True), "iterate_first", (got, peak, x) + (() if w is None else (w,)), [columns, messages, vec, vec], scratch)
    got = share(send)
    for _ in range(ITERS - 1):
        col, send = call(functools.partial(body, first=False), "iterate", (got, factor, w, x), [columns, messages], scratch)
        got = share(send)
    grad, load = call(
        functools.partial(final_body, size=size, balance=balance, kb=kb),
        "finish",
        (me1, got, factor, w, x, col, codebook, *segments),
        [jax.ShapeDtypeStruct((kl, d), jnp.float32), columns],
        [
            rows_f32,
            pltpu.VMEM((n, d), jnp.bfloat16),
            pltpu.VMEM((n // block, block // LANES, LANES), jnp.float32),
            pltpu.VMEM((kl, d), jnp.float32),
            pltpu.SemaphoreType.DMA((kl // kb,)),
        ],
        [pl.BlockSpec(memory_space=pl.ANY), IN_VMEM],
    )
    return grad, load.reshape(kl)


def solution(mesh):
    placed = (P("rows", None), P(("code", "rows"), None), P("rows"))
    return jax.shard_map(
        local,
        mesh=mesh,
        in_specs=placed,
        out_specs=(P(("code", "rows"), None), P(("code", "rows"))),
        check_vma=False,
    )
```

time: 116 us -> 102 us (0.88)
  waiting for transfers between devices: 12.4 us -> 5.62 us
  Pallas kernels: 35.2 us -> 30.8 us
  blocking collectives: 53.2 us -> 49.8 us
  starting transfers between devices: 8.99 us -> 11.9 us
  local copies, waits for them, and re-layouts: 5.48 us -> 2.83 us
    ppermute x7 -> x11, waiting for transfers between devices: 12.4 us -> 5.62 us  [exchange(): return lax.ppermute(x, AXES, [(i, i ^ mask) for i in range(size)])]
    pallas_call x5 -> x10, Pallas kernels: 35.2 us -> 30.8 us  [call(): pl.pallas_call(body, in_specs=[IN_SMEM if a.dtype == jnp.int32 else IN_VM...]
    all_to_all x1, blocking collectives: 18 us -> 13.7 us  [share_first(): lax.all_to_all(message, AXES, split_axis=0, concat_axis=0, tiled=True, ax...]
    ppermute x7 -> x11, starting transfers between devices: 8.99 us -> 11.9 us  [exchange(): return lax.ppermute(x, AXES, [(i, i ^ mask) for i in range(size)])]
    unnamed x11 -> x8, local copies, waits for them, and re-layouts: 4.73 us -> 2.83 us
  transfers between devices with their start and end apart: 7 -> 11, of which waited for: 5 -> 4; matrix products, arithmetic and copies ran while one was open for 3% -> 0% of each run, Pallas kernels for 0% -> 8%
where the time goes in v3:
time: 102 us
  blocking collectives  49.8 us (49%)
  Pallas kernels  30.8 us (30%)
  starting transfers between devices  11.9 us (12%)
  waiting for transfers between devices  5.62 us (6%)
  local copies, waits for them, and re-layouts  2.83 us (3%)
    all_to_all x3, blocking collectives, share(): return lax.all_to_all(send, AXES, split_axis=0, concat_axis=0, tiled=True)  36.1 us
    pallas_call x10, Pallas kernels, call(): pl.pallas_call(body, in_specs=[IN_SMEM if a.dtype == jnp.int32 else IN_VM...  30.8 us
    all_to_all x1, blocking collectives, share_first(): lax.all_to_all(message, AXES, split_axis=0, concat_axis=0, tiled=True, ax...  13.7 us
    ppermute x11, starting transfers between devices, exchange(): return lax.ppermute(x, AXES, [(i, i ^ mask) for i in range(size)])  11.9 us
    ppermute x11, waiting for transfers between devices, exchange(): return lax.ppermute(x, AXES, [(i, i ^ mask) for i in range(size)])  5.62 us
    unnamed x8, local copies, waits for them, and re-layouts  2.83 us
  transfers between devices with their start and end apart: 11, of which 4 were waited for; matrix products, arithmetic and copies ran while one was open for 0% of the time, Pallas kernels for 8%

profile of v3, /device:TPU:1, one launch (start us, length us, event | category | flops | bytes accessed | tf_op | source)
XLA Modules:
  0.0 101.8 jit_solution(11018020280187383324)
XLA Ops:
  0.6 0.0 copy-start
  0.6 0.9 copy-done
  1.6 4.2 %collective-permute-start.2 = (bf16[1,96,256]{2,1,0:T(8,128)(2,1)S(1)}, bf16[1,96,256]{2,1,0:T(8,128)(2,1)S(1)}, u32[]{:S(2)}, u32[]{:S(2)}) collective-permute-start(bf16[1,96,256]{2,1,0:T(8,128)(2,1)S(1)} %dynamic-slice_bitcast_fusion), channel_id=1, source_target_pairs={{0,24},{1,25},{2,26},{3,27},{4,28},{5,29},{6,30},{7,31},{8,16},{9,... | collective-permute-start | bytes 147464 | tf_op jit(solution)/shard_map/ppermute | solution.py:28
  5.7 0.0 collective-permute-start.1
  5.7 0.3 collective-permute-start
  6.1 1.2 %collective-permute-done.2 = bf16[1,96,256]{2,1,0:T(8,128)(2,1)S(1)} collective-permute-done((bf16[1,96,256]{2,1,0:T(8,128)(2,1)S(1)}, bf16[1,96,256]{2,1,0:T(8,128)(2,1)S(1)}, u32[]{:S(2)}, u32[]{:S(2)}) %collective-permute-start.2) | collective-permute-done | bytes 49184 | tf_op jit(solution)/shard_map/ppermute | solution.py:28
  7.2 2.9 %collective-permute-done.1 = bf16[1,96,256]{2,1,0:T(8,128)(2,1)S(1)} collective-permute-done((bf16[1,96,256]{2,1,0:T(8,128)(2,1)S(1)}, bf16[1,96,256]{2,1,0:T(8,128)(2,1)S(1)}, u32[]{:S(2)}, u32[]{:S(2)}) %collective-permute-start.1) | collective-permute-done | bytes 49184 | tf_op jit(solution)/shard_map/ppermute | solution.py:28
  10.1 0.0 collective-permute-done
  10.1 1.6 %collective-permute-start.6 = (bf16[1,4,96,256]{3,2,1,0:T(8,128)(2,1)S(1)}, bf16[1,4,96,256]{3,2,1,0:T(8,128)(2,1)S(1)}, u32[]{:S(2)}, u32[]{:S(2)}) collective-permute-start(bf16[1,4,96,256]{3,2,1,0:T(8,128)(2,1)S(1)} %maximum_bitcast_fusion.refs_3_.refs_7_), channel_id=1, source_target_pairs={{0,1},{1,0},{2,3},{3,2},{4,5},{5,4},{6,7},{7,6},{8,9},{9,8},{10,11... | collective-permute-start | bytes 589832 | tf_op jit(solution)/shard_map/ppermute | solution.py:28
  11.8 1.3 %collective-permute-start.5 = (bf16[1,4,96,256]{3,2,1,0:T(8,128)(2,1)S(1)}, bf16[1,4,96,256]{3,2,1,0:T(8,128)(2,1)S(1)}, u32[]{:S(2)}, u32[]{:S(2)}) collective-permute-start(bf16[1,4,96,256]{3,2,1,0:T(8,128)(2,1)S(1)} %maximum_bitcast_fusion.refs_3_.refs_7_), channel_id=1, source_target_pairs={{0,4},{1,5},{2,6},{3,7},{4,0},{5,1},{6,2},{7,3},{8,12},{9,13},{10,... | collective-permute-start | bytes 589832 | tf_op jit(solution)/shard_map/ppermute | solution.py:28
  13.0 1.2 %collective-permute-start.4 = (bf16[1,4,96,256]{3,2,1,0:T(8,128)(2,1)S(1)}, bf16[1,4,96,256]{3,2,1,0:T(8,128)(2,1)S(1)}, u32[]{:S(2)}, u32[]{:S(2)}) collective-permute-start(bf16[1,4,96,256]{3,2,1,0:T(8,128)(2,1)S(1)} %maximum_bitcast_fusion.refs_3_.refs_7_), channel_id=1, source_target_pairs={{0,2},{1,3},{2,0},{3,1},{4,6},{5,7},{6,4},{7,5},{8,10},{9,11},{10,... | collective-permute-start | bytes 589832 | tf_op jit(solution)/shard_map/ppermute | solution.py:28
  14.2 0.2 collective-permute-start.3
  14.4 0.0 collective-permute-done.6.refs_4_.refs_11_
  14.4 0.0 copy-start.1
  14.4 1.2 %copy-done.1 = bf16[2048,256]{1,0:T(8,128)(2,1)S(1)} copy-done((bf16[2048,256]{1,0:T(8,128)(2,1)S(1)}, bf16[2048,256]{1,0:T(8,128)(2,1)}, u32[]{:S(2)}) %copy-start.1) | copy-done | bytes 1048600
  15.7 0.0 copy-start.3
  15.7 0.7 copy-done.3
  16.3 2.4 %exponents.5 = (bf16[2048,3072]{1,0:T(8,128)(2,1)S(1)}, f32[24,128]{1,0:T(8,128)S(1)}, f32[27,128]{1,0:T(8,128)S(1)}) custom-call(s32[1]{0:T(128)} %bitcast.refs_0_.me_ref, f32[384]{0:T(512)S(1)} %copy-done.3, bf16[2048,256]{1,0:T(8,128)(2,1)S(1)} %copy-done.1, bf16[1,4,96,256]{3,2,1,0:T(8,128)(2,1)S(1)} %maximum_bitcast_fusion.refs_3_.refs_7_, ...), custom_call_target="tpu_custom_call" | custom-call | flops 805306368 | bytes 9437184 | tf_op jit(solution)/shard_map/exponents/pallas_call | solution.py:308
  18.7 0.0 collective-permute-done.5.refs_4_
  18.7 0.4 collective-permute-done.4.refs_3_
  19.2 2.4 %exponents.6 = (bf16[2048,3072]{1,0:T(8,128)(2,1)S(1)}, f32[24,128]{1,0:T(8,128)S(1)}, f32[27,128]{1,0:T(8,128)S(1)}, bf16[1,4,96,256]{3,2,1,0:T(8,128)(2,1)S(1)}, bf16[1,4,96,256]{3,2,1,0:T(8,128)(2,1)S(1)}) custom-call(s32[1]{0:T(128)} %bitcast.refs_0_.me_ref, ...), custom_call_target="tpu_custom_call", output_to_operand_aliasing={{3}: (3, {}), {4}: (4, {}), {0}: (5, {}), {1}: (6, {}), {2}... | custom-call | flops 805306368 | bytes 9437184 | tf_op jit(solution)/shard_map/exponents/pallas_call | solution.py:308
  21.6 2.0 %collective-permute-start.8 = (bf16[1,4,96,256]{3,2,1,0:T(8,128)(2,1)S(1)}, bf16[1,4,96,256]{3,2,1,0:T(8,128)(2,1)S(1)}, u32[]{:S(2)}, u32[]{:S(2)}) collective-permute-start(bf16[1,4,96,256]{3,2,1,0:T(8,128)(2,1)S(1)} %get-tuple-element.35.refs_8_), channel_id=1, source_target_pairs={{0,1},{1,0},{2,3},{3,2},{4,5},{5,4},{6,7},{7,6},{8,9},{9,8},{10,11... | collective-permute-start | bytes 589832 | tf_op jit(solution)/shard_map/ppermute | solution.py:28
  23.6 0.1 collective-permute-start.9
  23.6 0.0 collective-permute-done.3.refs_3_
  23.7 1.3 %exponents.7 = (bf16[2048,3072]{1,0:T(8,128)(2,1)S(1)}, f32[24,128]{1,0:T(8,128)S(1)}, f32[27,128]{1,0:T(8,128)S(1)}, bf16[1,4,96,256]{3,2,1,0:T(8,128)(2,1)S(1)}) custom-call(s32[1]{0:T(128)} %bitcast.refs_0_.me_ref, f32[384]{0:T(512)S(1)} %copy-done.3, ...), custom_call_target="tpu_custom_call", output_to_operand_aliasing={{3}: (3, {}), {0}: (4, {}), {1}: (5, {}), {2}: (6, {})} | custom-call | flops 402653184 | bytes 4718592 | tf_op jit(solution)/shard_map/exponents/pallas_call | solution.py:308
  24.9 0.9 collective-permute-start.7
  25.8 0.0 collective-permute-done.8.refs_3_.refs_12_
  25.8 0.0 collective-permute-done.9.refs_4_.refs_13_
  25.8 2.4 %exponents.8 = (bf16[2048,3072]{1,0:T(8,128)(2,1)S(1)}, f32[24,128]{1,0:T(8,128)S(1)}, f32[27,128]{1,0:T(8,128)S(1)}) custom-call(s32[1]{0:T(128)} %bitcast.refs_0_.me_ref, f32[384]{0:T(512)S(1)} %copy-done.3, bf16[2048,256]{1,0:T(8,128)(2,1)S(1)} %copy-done.1, ...), custom_call_target="tpu_custom_call", output_to_operand_aliasing={{0}: (5, {}), {1}: (6, {}), {2}: (7, {})} | custom-call | flops 805306368 | bytes 9437184 | tf_op jit(solution)/shard_map/exponents/pallas_call | solution.py:308
  28.3 0.0 collective-permute-done.7.refs_3_.refs_14_
  28.3 1.3 %exponents.9 = (bf16[2048,3072]{1,0:T(8,128)(2,1)S(1)}, f32[24,128]{1,0:T(8,128)S(1)}, f32[27,128]{1,0:T(8,128)S(1)}) custom-call(s32[1]{0:T(128)} %bitcast.refs_0_.me_ref, f32[384]{0:T(512)S(1)} %copy-done.3, bf16[2048,256]{1,0:T(8,128)(2,1)S(1)} %copy-done.1, ...), custom_call_target="tpu_custom_call", output_to_operand_aliasing={{0}: (4, {}), {1}: (5, {}), {2}: (6, {})} | custom-call | flops 402653184 | bytes 4718592 | tf_op jit(solution)/shard_map/exponents/pallas_call | solution.py:308
  29.6 0.1 collective-permute-start.10
  29.7 1.2 %collective-permute-done.10.other_ref = f32[27,128]{1,0:T(8,128)S(1)} collective-permute-done((f32[27,128]{1,0:T(8,128)S(1)}, f32[27,128]{1,0:T(8,128)S(1)}, u32[]{:S(2)}, u32[]{:S(2)}) %collective-permute-start.10) | collective-permute-done | bytes 13856 | tf_op jit(solution)/shard_map/ppermute | solution.py:28
  30.8 13.7 %all_to_all.20.refs_0_ = f32[16,30,128]{2,1,0:T(8,128)S(1)} all-to-all(f32[16,30,128]{2,1,0:T(8,128)S(1)} %join.1), channel_id=1, replica_groups={{0,2,4,6,8,10,12,14,16,18,20,22,24,26,28,30},{1,3,5,7,9,11,13,15,17,19,..., dimensions={0} | all-to-all | bytes 491520 | tf_op jit(solution)/shard_map/all_to_all | solution.py:281
  44.6 4.3 %iterate_first.1 = (f32[1,2048]{1,0:T(1,128)}, bf16[32,24,128]{2,1,0:T(8,128)(2,1)S(1)}, f32[24,128]{1,0:T(8,128)S(1)}, f32[24,128]{1,0:T(8,128)S(1)}) custom-call(f32[16,30,128]{2,1,0:T(8,128)S(1)} %all_to_all.20.refs_0_, f32[24,128]{1,0:T(8,128)S(1)} %get-tuple-element.44.refs_1_, bf16[2048,3072]{1,0:T(8,128)(2,1)S(1)} %get-tuple-element.45.refs_2_.refs_3_.refs_4_), custom_call_target="tpu_custom_call" | custom-call | tf_op jit(solution)/shard_map/iterate_first/pallas_call | solution.py:308
  48.8 13.3 %all_to_all.21.refs_0_ = bf16[32,24,128]{2,1,0:T(8,128)(2,1)S(1)} all-to-all(bf16[32,24,128]{2,1,0:T(8,128)(2,1)S(1)} %get-tuple-element.46), channel_id=1, replica_groups=mesh['rows'=8,'code'=4] {'rows','code'}, dimensions={0} | all-to-all | bytes 393216 | tf_op jit(solution)/shard_map/all_to_all | solution.py:296
  62.1 0.0 copy-start.2
  62.1 4.3 %iterate.2 = (f32[1,2048]{1,0:T(1,128)}, bf16[32,24,128]{2,1,0:T(8,128)(2,1)S(1)}) custom-call(bf16[32,24,128]{2,1,0:T(8,128)(2,1)S(1)} %all_to_all.21.refs_0_, f32[24,128]{1,0:T(8,128)S(1)} %get-tuple-element.47.refs_1_.refs_2_, f32[24,128]{1,0:T(8,128)S(1)} %get-tuple-element.48.refs_2_.refs_3_, ...), custom_call_target="tpu_custom_call" | custom-call | tf_op jit(solution)/shard_map/iterate/pallas_call | solution.py:308
  66.4 11.4 %all_to_all.22.refs_0_ = bf16[32,24,128]{2,1,0:T(8,128)(2,1)S(1)} all-to-all(bf16[32,24,128]{2,1,0:T(8,128)(2,1)S(1)} %get-tuple-element.49), channel_id=1, replica_groups=mesh['rows'=8,'code'=4] {'rows','code'}, dimensions={0} | all-to-all | bytes 393216 | tf_op jit(solution)/shard_map/all_to_all | solution.py:296
  77.8 4.1 %iterate.3 = (f32[1,2048]{1,0:T(1,128)S(1)}, bf16[32,24,128]{2,1,0:T(8,128)(2,1)S(1)}) custom-call(bf16[32,24,128]{2,1,0:T(8,128)(2,1)S(1)} %all_to_all.22.refs_0_, f32[24,128]{1,0:T(8,128)S(1)} %get-tuple-element.47.refs_1_.refs_2_, f32[24,128]{1,0:T(8,128)S(1)} %get-tuple-element.48.refs_2_.refs_3_, ...), custom_call_target="tpu_custom_call" | custom-call | tf_op jit(solution)/shard_map/iterate/pallas_call | solution.py:308
  81.9 11.4 %all_to_all.23.refs_1_ = bf16[32,24,128]{2,1,0:T(8,128)(2,1)S(1)} all-to-all(bf16[32,24,128]{2,1,0:T(8,128)(2,1)S(1)} %get-tuple-element.50), channel_id=1, replica_groups=mesh['rows'=8,'code'=4] {'rows','code'}, dimensions={0} | all-to-all | bytes 393216 | tf_op jit(solution)/shard_map/all_to_all | solution.py:296
  93.3 0.0 copy-done.2
  93.3 8.3 %finish.1 = (f32[2048,256]{1,0:T(8,128)}, f32[1,2048]{1,0:T(1,128)}) custom-call(s32[1]{0:T(128)} %bitcast.refs_0_.me_ref, bf16[32,24,128]{2,1,0:T(8,128)(2,1)S(1)} %all_to_all.23.refs_1_, f32[24,128]{1,0:T(8,128)S(1)} %get-tuple-element.47.refs_1_.refs_2_, f32[24,128]{1,0:T(8,128)S(1)} %get-tuple-element.48.refs_2_.refs_3_, ...), custom_call_target="tpu_custom_call" | custom-call | tf_op jit(solution)/shard_map/finish/pallas_call | solution.py:308
  (3 shorter events, 0.1 us)
Async XLA Ops:
  0.6 0.9 copy-start
  1.6 5.7 %collective-permute-start.2 = (bf16[1,96,256]{2,1,0:T(8,128)(2,1)S(1)}, bf16[1,96,256]{2,1,0:T(8,128)(2,1)S(1)}, u32[]{:S(2)}, u32[]{:S(2)}) collective-permute-start(bf16[1,96,256]{2,1,0:T(8,128)(2,1)S(1)} %dynamic-slice_bitcast_fusion), channel_id=1, source_target_pairs={{0,24},{1,25},{2,26},{3,27},{4,28},{5,29},{6,30},{7,31},{8,16},{9,... | collective-permute-start | bytes 147464 | tf_op jit(solution)/shard_map/ppermute | solution.py:28
  5.7 4.4 %collective-permute-start.1 = (bf16[1,96,256]{2,1,0:T(8,128)(2,1)S(1)}, bf16[1,96,256]{2,1,0:T(8,128)(2,1)S(1)}, u32[]{:S(2)}, u32[]{:S(2)}) collective-permute-start(bf16[1,96,256]{2,1,0:T(8,128)(2,1)S(1)} %dynamic-slice_bitcast_fusion), channel_id=1, source_target_pairs={{0,16},{1,17},{2,18},{3,19},{4,20},{5,21},{6,22},{7,23},{8,24},{9,... | collective-permute-start | bytes 147464 | tf_op jit(solution)/shard_map/ppermute | solution.py:28
  5.7 4.4 %collective-permute-start = (bf16[1,96,256]{2,1,0:T(8,128)(2,1)S(1)}, bf16[1,96,256]{2,1,0:T(8,128)(2,1)S(1)}, u32[]{:S(2)}, u32[]{:S(2)}) collective-permute-start(bf16[1,96,256]{2,1,0:T(8,128)(2,1)S(1)} %dynamic-slice_bitcast_fusion), channel_id=1, source_target_pairs={{0,8},{1,9},{2,10},{3,11},{4,12},{5,13},{6,14},{7,15},{8,0},{9,1},... | collective-permute-start | bytes 147464 | tf_op jit(solution)/shard_map/ppermute | solution.py:28
  10.1 4.3 %collective-permute-start.6 = (bf16[1,4,96,256]{3,2,1,0:T(8,128)(2,1)S(1)}, bf16[1,4,96,256]{3,2,1,0:T(8,128)(2,1)S(1)}, u32[]{:S(2)}, u32[]{:S(2)}) collective-permute-start(bf16[1,4,96,256]{3,2,1,0:T(8,128)(2,1)S(1)} %maximum_bitcast_fusion.refs_3_.refs_7_), channel_id=1, source_target_pairs={{0,1},{1,0},{2,3},{3,2},{4,5},{5,4},{6,7},{7,6},{8,9},{9,8},{10,11... | collective-permute-start | bytes 589832 | tf_op jit(solution)/shard_map/ppermute | solution.py:28
  11.8 7.0 %collective-permute-start.5 = (bf16[1,4,96,256]{3,2,1,0:T(8,128)(2,1)S(1)}, bf16[1,4,96,256]{3,2,1,0:T(8,128)(2,1)S(1)}, u32[]{:S(2)}, u32[]{:S(2)}) collective-permute-start(bf16[1,4,96,256]{3,2,1,0:T(8,128)(2,1)S(1)} %maximum_bitcast_fusion.refs_3_.refs_7_), channel_id=1, source_target_pairs={{0,4},{1,5},{2,6},{3,7},{4,0},{5,1},{6,2},{7,3},{8,12},{9,13},{10,... | collective-permute-start | bytes 589832 | tf_op jit(solution)/shard_map/ppermute | solution.py:28
  13.0 6.1 %collective-permute-start.4 = (bf16[1,4,96,256]{3,2,1,0:T(8,128)(2,1)S(1)}, bf16[1,4,96,256]{3,2,1,0:T(8,128)(2,1)S(1)}, u32[]{:S(2)}, u32[]{:S(2)}) collective-permute-start(bf16[1,4,96,256]{3,2,1,0:T(8,128)(2,1)S(1)} %maximum_bitcast_fusion.refs_3_.refs_7_), channel_id=1, source_target_pairs={{0,2},{1,3},{2,0},{3,1},{4,6},{5,7},{6,4},{7,5},{8,10},{9,11},{10,... | collective-permute-start | bytes 589832 | tf_op jit(solution)/shard_map/ppermute | solution.py:28
  14.2 9.4 %collective-permute-start.3 = (bf16[1,4,96,256]{3,2,1,0:T(8,128)(2,1)S(1)}, bf16[1,4,96,256]{3,2,1,0:T(8,128)(2,1)S(1)}, u32[]{:S(2)}, u32[]{:S(2)}) collective-permute-start(bf16[1,4,96,256]{3,2,1,0:T(8,128)(2,1)S(1)} %maximum_bitcast_fusion.refs_3_.refs_7_), channel_id=1, source_target_pairs={{0,6},{1,7},{2,4},{3,5},{4,2},{5,3},{6,0},{7,1},{8,14},{9,15},{10,... | collective-permute-start | bytes 589832 | tf_op jit(solution)/shard_map/ppermute | solution.py:28
  14.4 1.2 %copy-start.1 = (bf16[2048,256]{1,0:T(8,128)(2,1)S(1)}, bf16[2048,256]{1,0:T(8,128)(2,1)}, u32[]{:S(2)}) copy-start(bf16[2048,256]{1,0:T(8,128)(2,1)} %refs_6_.1) | copy-start | bytes 3145732
  15.7 0.7 copy-start.3
  21.6 4.3 %collective-permute-start.8 = (bf16[1,4,96,256]{3,2,1,0:T(8,128)(2,1)S(1)}, bf16[1,4,96,256]{3,2,1,0:T(8,128)(2,1)S(1)}, u32[]{:S(2)}, u32[]{:S(2)}) collective-permute-start(bf16[1,4,96,256]{3,2,1,0:T(8,128)(2,1)S(1)} %get-tuple-element.35.refs_8_), channel_id=1, source_target_pairs={{0,1},{1,0},{2,3},{3,2},{4,5},{5,4},{6,7},{7,6},{8,9},{9,8},{10,11... | collective-permute-start | bytes 589832 | tf_op jit(solution)/shard_map/ppermute | solution.py:28
  23.6 2.3 %collective-permute-start.9 = (bf16[1,4,96,256]{3,2,1,0:T(8,128)(2,1)S(1)}, bf16[1,4,96,256]{3,2,1,0:T(8,128)(2,1)S(1)}, u32[]{:S(2)}, u32[]{:S(2)}) collective-permute-start(bf16[1,4,96,256]{3,2,1,0:T(8,128)(2,1)S(1)} %get-tuple-element.36.refs_9_), channel_id=1, source_target_pairs={{0,1},{1,0},{2,3},{3,2},{4,5},{5,4},{6,7},{7,6},{8,9},{9,8},{10,11... | collective-permute-start | bytes 589832 | tf_op jit(solution)/shard_map/ppermute | solution.py:28
  24.9 3.3 %collective-permute-start.7 = (bf16[1,4,96,256]{3,2,1,0:T(8,128)(2,1)S(1)}, bf16[1,4,96,256]{3,2,1,0:T(8,128)(2,1)S(1)}, u32[]{:S(2)}, u32[]{:S(2)}) collective-permute-start(bf16[1,4,96,256]{3,2,1,0:T(8,128)(2,1)S(1)} %get-tuple-element.34.refs_10_), channel_id=1, source_target_pairs={{0,1},{1,0},{2,3},{3,2},{4,5},{5,4},{6,7},{7,6},{8,9},{9,8},{10,11... | collective-permute-start | bytes 589832 | tf_op jit(solution)/shard_map/ppermute | solution.py:28
  29.6 1.2 %collective-permute-start.10 = (f32[27,128]{1,0:T(8,128)S(1)}, f32[27,128]{1,0:T(8,128)S(1)}, u32[]{:S(2)}, u32[]{:S(2)}) collective-permute-start(f32[27,128]{1,0:T(8,128)S(1)} %get-tuple-element.43.own_ref), channel_id=1, source_target_pairs={{0,1},{1,0},{2,3},{3,2},{4,5},{5,4},{6,7},{7,6},{8,9},{9,8},{10,11... | collective-permute-start | bytes 41480 | tf_op jit(solution)/shard_map/ppermute | solution.py:28
  62.1 31.2 %copy-start.2 = (bf16[2048,256]{1,0:T(8,128)(2,1)S(1)}, bf16[2048,256]{1,0:T(8,128)(2,1)}, u32[]{:S(2)}) copy-start(bf16[2048,256]{1,0:T(8,128)(2,1)} %refs_6_.1) | copy-start | bytes 3145732

commit v4 on v3

--- a/solution.py
+++ b/solution.py
@@ -140,18 +140,25 @@
 
 def put_rows(dst, r):
     for t in range(r.shape[0]):
-        dst[:, t * LANES : (t + 1) * LANES] = jnp.broadcast_to(r[t : t + 1, :], (8, LANES))
+        dst[:, t * LANES : (t + 1) * LANES] = jnp.broadcast_to(r[t : t + 1, :], (16, LANES)).astype(jnp.bfloat16)
 
 
 def column_sums(x_ref, r_ref, k, kb):
+    tiles = r_ref.shape[1] // LANES
+    join = 4 if tiles % 4 == 0 else 1
     parts = []
     for g in range(k, k + kb, 16):
-        sums = [None, None]
-        for t in range(r_ref.shape[1] // LANES):
-            lanes = slice(t * LANES, (t + 1) * LANES)
-            term = x_ref[g : g + 16, lanes].astype(jnp.float32) * jnp.broadcast_to(r_ref[0:1, lanes], (16, LANES))
-            sums[t % 2] = term if sums[t % 2] is None else sums[t % 2] + term
-        parts.append(sums[0] + sums[1])
+        total = None
+        for t in range(0, tiles, join):
+            terms = []
+            for u in range(t, t + join):
+                lanes = slice(u * LANES, (u + 1) * LANES)
+                terms.append(x_ref[g : g + 16, lanes] * r_ref[:, lanes])
+            while len(terms) > 1:
+                terms = [terms[i] + terms[i + 1] for i in range(0, len(terms), 2)]
+            term = terms[0].astype(jnp.float32)
+            total = term if total is None else total + term
+        parts.append(total)
     return jnp.sum(jnp.concatenate(parts, axis=0).T, axis=0, keepdims=True)
 
 
@@ -376,9 +383,9 @@
     x, peak, lse = state
     x = pltpu.with_memory_space_constraint(x, pltpu.VMEM)
     got, w, plan = share_first(lse, weights, me1, size, copies, nt)
-    rows_f32 = pltpu.VMEM((8, n), jnp.float32)
+    row_scales = pltpu.VMEM((16, n), jnp.bfloat16)
     kb = min(256, kl)
-    scratch = [rows_f32, pltpu.VMEM((16, n), jnp.float32)]
+    scratch = [row_scales, pltpu.VMEM((16, n), jnp.float32)]
     messages = jax.ShapeDtypeStruct((copies, nt, LANES), jnp.bfloat16)
     columns = jax.ShapeDtypeStruct((1, kl), jnp.float32)
     body = functools.partial(iterate_body, balance=balance, kb=kb, plan=plan)
@@ -393,7 +400,7 @@
         (me1, got, factor, w, x, col, codebook, *segments),
         [jax.ShapeDtypeStruct((kl, d), jnp.float32), columns],
         [
-            rows_f32,
+            row_scales,
             pltpu.VMEM((n, d), jnp.bfloat16),
             pltpu.VMEM((n // block, block // LANES, LANES), jnp.float32),
             pltpu.VMEM((kl, d), jnp.float32),

time: 102 us -> 101 us (level)
  Pallas kernels: 30.8 us -> 29.6 us
    pallas_call x10, Pallas kernels: 30.8 us -> 29.6 us  [call(): pl.pallas_call(body, in_specs=[IN_SMEM if a.dtype == jnp.int32 else IN_VM...]
where the time goes in v4:
time: 101 us
  blocking collectives  49.8 us (49%)
  Pallas kernels  29.6 us (29%)
  starting transfers between devices  11.9 us (12%)
  waiting for transfers between devices  5.62 us (6%)
  local copies, waits for them, and re-layouts  2.83 us (3%)
    all_to_all x3, blocking collectives, share(): return lax.all_to_all(send, AXES, split_axis=0, concat_axis=0, tiled=True)  36.1 us
    pallas_call x10, Pallas kernels, call(): pl.pallas_call(body, in_specs=[IN_SMEM if a.dtype == jnp.int32 else IN_VM...  29.6 us
    all_to_all x1, blocking collectives, share_first(): lax.all_to_all(message, AXES, split_axis=0, concat_axis=0, tiled=True, ax...  13.7 us
    ppermute x11, starting transfers between devices, exchange(): return lax.ppermute(x, AXES, [(i, i ^ mask) for i in range(size)])  11.9 us
    ppermute x11, waiting for transfers between devices, exchange(): return lax.ppermute(x, AXES, [(i, i ^ mask) for i in range(size)])  5.62 us
    unnamed x8, local copies, waits for them, and re-layouts  2.83 us
  transfers between devices with their start and end apart: 11, of which 4 were waited for; matrix products, arithmetic and copies ran while one was open for 0% of the time, Pallas kernels for 8%

profile of v4, /device:TPU:1, one launch (start us, length us, event | category | flops | bytes accessed | tf_op | source)
XLA Modules:
  0.0 100.6 jit_solution(4168331390756131294)
XLA Ops:
  0.6 0.0 copy-start
  0.6 0.9 copy-done
  1.6 4.2 %collective-permute-start.2 = (bf16[1,96,256]{2,1,0:T(8,128)(2,1)S(1)}, bf16[1,96,256]{2,1,0:T(8,128)(2,1)S(1)}, u32[]{:S(2)}, u32[]{:S(2)}) collective-permute-start(bf16[1,96,256]{2,1,0:T(8,128)(2,1)S(1)} %dynamic-slice_bitcast_fusion), channel_id=1, source_target_pairs={{0,24},{1,25},{2,26},{3,27},{4,28},{5,29},{6,30},{7,31},{8,16},{9,... | collective-permute-start | bytes 147464 | tf_op jit(solution)/shard_map/ppermute | solution.py:28
  5.7 0.0 collective-permute-start.1
  5.7 0.3 collective-permute-start
  6.1 1.2 %collective-permute-done.2 = bf16[1,96,256]{2,1,0:T(8,128)(2,1)S(1)} collective-permute-done((bf16[1,96,256]{2,1,0:T(8,128)(2,1)S(1)}, bf16[1,96,256]{2,1,0:T(8,128)(2,1)S(1)}, u32[]{:S(2)}, u32[]{:S(2)}) %collective-permute-start.2) | collective-permute-done | bytes 49184 | tf_op jit(solution)/shard_map/ppermute | solution.py:28
  7.2 2.9 %collective-permute-done.1 = bf16[1,96,256]{2,1,0:T(8,128)(2,1)S(1)} collective-permute-done((bf16[1,96,256]{2,1,0:T(8,128)(2,1)S(1)}, bf16[1,96,256]{2,1,0:T(8,128)(2,1)S(1)}, u32[]{:S(2)}, u32[]{:S(2)}) %collective-permute-start.1) | collective-permute-done | bytes 49184 | tf_op jit(solution)/shard_map/ppermute | solution.py:28
  10.1 0.0 collective-permute-done
  10.1 1.6 %collective-permute-start.6 = (bf16[1,4,96,256]{3,2,1,0:T(8,128)(2,1)S(1)}, bf16[1,4,96,256]{3,2,1,0:T(8,128)(2,1)S(1)}, u32[]{:S(2)}, u32[]{:S(2)}) collective-permute-start(bf16[1,4,96,256]{3,2,1,0:T(8,128)(2,1)S(1)} %maximum_bitcast_fusion.refs_3_.refs_7_), channel_id=1, source_target_pairs={{0,1},{1,0},{2,3},{3,2},{4,5},{5,4},{6,7},{7,6},{8,9},{9,8},{10,11... | collective-permute-start | bytes 589832 | tf_op jit(solution)/shard_map/ppermute | solution.py:28
  11.8 1.3 %collective-permute-start.5 = (bf16[1,4,96,256]{3,2,1,0:T(8,128)(2,1)S(1)}, bf16[1,4,96,256]{3,2,1,0:T(8,128)(2,1)S(1)}, u32[]{:S(2)}, u32[]{:S(2)}) collective-permute-start(bf16[1,4,96,256]{3,2,1,0:T(8,128)(2,1)S(1)} %maximum_bitcast_fusion.refs_3_.refs_7_), channel_id=1, source_target_pairs={{0,4},{1,5},{2,6},{3,7},{4,0},{5,1},{6,2},{7,3},{8,12},{9,13},{10,... | collective-permute-start | bytes 589832 | tf_op jit(solution)/shard_map/ppermute | solution.py:28
  13.0 1.2 %collective-permute-start.4 = (bf16[1,4,96,256]{3,2,1,0:T(8,128)(2,1)S(1)}, bf16[1,4,96,256]{3,2,1,0:T(8,128)(2,1)S(1)}, u32[]{:S(2)}, u32[]{:S(2)}) collective-permute-start(bf16[1,4,96,256]{3,2,1,0:T(8,128)(2,1)S(1)} %maximum_bitcast_fusion.refs_3_.refs_7_), channel_id=1, source_target_pairs={{0,2},{1,3},{2,0},{3,1},{4,6},{5,7},{6,4},{7,5},{8,10},{9,11},{10,... | collective-permute-start | bytes 589832 | tf_op jit(solution)/shard_map/ppermute | solution.py:28
  14.2 0.2 collective-permute-start.3
  14.4 0.0 collective-permute-done.6.refs_4_.refs_11_
  14.4 0.0 copy-start.1
  14.4 1.2 %copy-done.1 = bf16[2048,256]{1,0:T(8,128)(2,1)S(1)} copy-done((bf16[2048,256]{1,0:T(8,128)(2,1)S(1)}, bf16[2048,256]{1,0:T(8,128)(2,1)}, u32[]{:S(2)}) %copy-start.1) | copy-done | bytes 1048600
  15.7 0.0 copy-start.3
  15.7 0.7 copy-done.3
  16.3 2.4 %exponents.5 = (bf16[2048,3072]{1,0:T(8,128)(2,1)S(1)}, f32[24,128]{1,0:T(8,128)S(1)}, f32[27,128]{1,0:T(8,128)S(1)}) custom-call(s32[1]{0:T(128)} %bitcast.refs_0_.me_ref, f32[384]{0:T(512)S(1)} %copy-done.3, bf16[2048,256]{1,0:T(8,128)(2,1)S(1)} %copy-done.1, bf16[1,4,96,256]{3,2,1,0:T(8,128)(2,1)S(1)} %maximum_bitcast_fusion.refs_3_.refs_7_, ...), custom_call_target="tpu_custom_call" | custom-call | flops 805306368 | bytes 9437184 | tf_op jit(solution)/shard_map/exponents/pallas_call | solution.py:315
  18.7 0.0 collective-permute-done.5.refs_4_
  18.7 0.4 collective-permute-done.4.refs_3_
  19.2 2.4 %exponents.6 = (bf16[2048,3072]{1,0:T(8,128)(2,1)S(1)}, f32[24,128]{1,0:T(8,128)S(1)}, f32[27,128]{1,0:T(8,128)S(1)}, bf16[1,4,96,256]{3,2,1,0:T(8,128)(2,1)S(1)}, bf16[1,4,96,256]{3,2,1,0:T(8,128)(2,1)S(1)}) custom-call(s32[1]{0:T(128)} %bitcast.refs_0_.me_ref, ...), custom_call_target="tpu_custom_call", output_to_operand_aliasing={{3}: (3, {}), {4}: (4, {}), {0}: (5, {}), {1}: (6, {}), {2}... | custom-call | flops 805306368 | bytes 9437184 | tf_op jit(solution)/shard_map/exponents/pallas_call | solution.py:315
  21.6 2.0 %collective-permute-start.8 = (bf16[1,4,96,256]{3,2,1,0:T(8,128)(2,1)S(1)}, bf16[1,4,96,256]{3,2,1,0:T(8,128)(2,1)S(1)}, u32[]{:S(2)}, u32[]{:S(2)}) collective-permute-start(bf16[1,4,96,256]{3,2,1,0:T(8,128)(2,1)S(1)} %get-tuple-element.35.refs_8_), channel_id=1, source_target_pairs={{0,1},{1,0},{2,3},{3,2},{4,5},{5,4},{6,7},{7,6},{8,9},{9,8},{10,11... | collective-permute-start | bytes 589832 | tf_op jit(solution)/shard_map/ppermute | solution.py:28
  23.6 0.1 collective-permute-start.9
  23.6 0.0 collective-permute-done.3.refs_3_
  23.7 1.3 %exponents.7 = (bf16[2048,3072]{1,0:T(8,128)(2,1)S(1)}, f32[24,128]{1,0:T(8,128)S(1)}, f32[27,128]{1,0:T(8,128)S(1)}, bf16[1,4,96,256]{3,2,1,0:T(8,128)(2,1)S(1)}) custom-call(s32[1]{0:T(128)} %bitcast.refs_0_.me_ref, f32[384]{0:T(512)S(1)} %copy-done.3, ...), custom_call_target="tpu_custom_call", output_to_operand_aliasing={{3}: (3, {}), {0}: (4, {}), {1}: (5, {}), {2}: (6, {})} | custom-call | flops 402653184 | bytes 4718592 | tf_op jit(solution)/shard_map/exponents/pallas_call | solution.py:315
  24.9 0.9 collective-permute-start.7
  25.8 0.0 collective-permute-done.8.refs_3_.refs_12_
  25.8 0.0 collective-permute-done.9.refs_4_.refs_13_
  25.8 2.4 %exponents.8 = (bf16[2048,3072]{1,0:T(8,128)(2,1)S(1)}, f32[24,128]{1,0:T(8,128)S(1)}, f32[27,128]{1,0:T(8,128)S(1)}) custom-call(s32[1]{0:T(128)} %bitcast.refs_0_.me_ref, f32[384]{0:T(512)S(1)} %copy-done.3, bf16[2048,256]{1,0:T(8,128)(2,1)S(1)} %copy-done.1, ...), custom_call_target="tpu_custom_call", output_to_operand_aliasing={{0}: (5, {}), {1}: (6, {}), {2}: (7, {})} | custom-call | flops 805306368 | bytes 9437184 | tf_op jit(solution)/shard_map/exponents/pallas_call | solution.py:315
  28.3 0.0 collective-permute-done.7.refs_3_.refs_14_
  28.3 1.3 %exponents.9 = (bf16[2048,3072]{1,0:T(8,128)(2,1)S(1)}, f32[24,128]{1,0:T(8,128)S(1)}, f32[27,128]{1,0:T(8,128)S(1)}) custom-call(s32[1]{0:T(128)} %bitcast.refs_0_.me_ref, f32[384]{0:T(512)S(1)} %copy-done.3, bf16[2048,256]{1,0:T(8,128)(2,1)S(1)} %copy-done.1, ...), custom_call_target="tpu_custom_call", output_to_operand_aliasing={{0}: (4, {}), {1}: (5, {}), {2}: (6, {})} | custom-call | flops 402653184 | bytes 4718592 | tf_op jit(solution)/shard_map/exponents/pallas_call | solution.py:315
  29.6 0.1 collective-permute-start.10
  29.7 1.2 %collective-permute-done.10.other_ref = f32[27,128]{1,0:T(8,128)S(1)} collective-permute-done((f32[27,128]{1,0:T(8,128)S(1)}, f32[27,128]{1,0:T(8,128)S(1)}, u32[]{:S(2)}, u32[]{:S(2)}) %collective-permute-start.10) | collective-permute-done | bytes 13856 | tf_op jit(solution)/shard_map/ppermute | solution.py:28
  30.8 13.7 %all_to_all.20.refs_0_ = f32[16,30,128]{2,1,0:T(8,128)S(1)} all-to-all(f32[16,30,128]{2,1,0:T(8,128)S(1)} %join.1), channel_id=1, replica_groups={{0,2,4,6,8,10,12,14,16,18,20,22,24,26,28,30},{1,3,5,7,9,11,13,15,17,19,..., dimensions={0} | all-to-all | bytes 491520 | tf_op jit(solution)/shard_map/all_to_all | solution.py:288
  44.6 4.0 %iterate_first.1 = (f32[1,2048]{1,0:T(1,128)}, bf16[32,24,128]{2,1,0:T(8,128)(2,1)S(1)}, f32[24,128]{1,0:T(8,128)S(1)}, f32[24,128]{1,0:T(8,128)S(1)}) custom-call(f32[16,30,128]{2,1,0:T(8,128)S(1)} %all_to_all.20.refs_0_, f32[24,128]{1,0:T(8,128)S(1)} %get-tuple-element.44.refs_1_, bf16[2048,3072]{1,0:T(8,128)(2,1)S(1)} %get-tuple-element.45.refs_2_.refs_3_.refs_4_), custom_call_target="tpu_custom_call" | custom-call | tf_op jit(solution)/shard_map/iterate_first/pallas_call | solution.py:315
  48.5 13.3 %all_to_all.21.refs_0_ = bf16[32,24,128]{2,1,0:T(8,128)(2,1)S(1)} all-to-all(bf16[32,24,128]{2,1,0:T(8,128)(2,1)S(1)} %get-tuple-element.46), channel_id=1, replica_groups=mesh['rows'=8,'code'=4] {'rows','code'}, dimensions={0} | all-to-all | bytes 393216 | tf_op jit(solution)/shard_map/all_to_all | solution.py:303
  61.8 0.0 copy-start.2
  61.8 3.9 %iterate.2 = (f32[1,2048]{1,0:T(1,128)}, bf16[32,24,128]{2,1,0:T(8,128)(2,1)S(1)}) custom-call(bf16[32,24,128]{2,1,0:T(8,128)(2,1)S(1)} %all_to_all.21.refs_0_, f32[24,128]{1,0:T(8,128)S(1)} %get-tuple-element.47.refs_1_.refs_2_, f32[24,128]{1,0:T(8,128)S(1)} %get-tuple-element.48.refs_2_.refs_3_, ...), custom_call_target="tpu_custom_call" | custom-call | tf_op jit(solution)/shard_map/iterate/pallas_call | solution.py:315
  65.7 11.4 %all_to_all.22.refs_0_ = bf16[32,24,128]{2,1,0:T(8,128)(2,1)S(1)} all-to-all(bf16[32,24,128]{2,1,0:T(8,128)(2,1)S(1)} %get-tuple-element.49), channel_id=1, replica_groups=mesh['rows'=8,'code'=4] {'rows','code'}, dimensions={0} | all-to-all | bytes 393216 | tf_op jit(solution)/shard_map/all_to_all | solution.py:303
  77.1 3.8 %iterate.3 = (f32[1,2048]{1,0:T(1,128)S(1)}, bf16[32,24,128]{2,1,0:T(8,128)(2,1)S(1)}) custom-call(bf16[32,24,128]{2,1,0:T(8,128)(2,1)S(1)} %all_to_all.22.refs_0_, f32[24,128]{1,0:T(8,128)S(1)} %get-tuple-element.47.refs_1_.refs_2_, f32[24,128]{1,0:T(8,128)S(1)} %get-tuple-element.48.refs_2_.refs_3_, ...), custom_call_target="tpu_custom_call" | custom-call | tf_op jit(solution)/shard_map/iterate/pallas_call | solution.py:315
  80.9 11.4 %all_to_all.23.refs_1_ = bf16[32,24,128]{2,1,0:T(8,128)(2,1)S(1)} all-to-all(bf16[32,24,128]{2,1,0:T(8,128)(2,1)S(1)} %get-tuple-element.50), channel_id=1, replica_groups=mesh['rows'=8,'code'=4] {'rows','code'}, dimensions={0} | all-to-all | bytes 393216 | tf_op jit(solution)/shard_map/all_to_all | solution.py:303
  92.4 0.0 copy-done.2
  92.4 8.1 %finish.1 = (f32[2048,256]{1,0:T(8,128)}, f32[1,2048]{1,0:T(1,128)}) custom-call(s32[1]{0:T(128)} %bitcast.refs_0_.me_ref, bf16[32,24,128]{2,1,0:T(8,128)(2,1)S(1)} %all_to_all.23.refs_1_, f32[24,128]{1,0:T(8,128)S(1)} %get-tuple-element.47.refs_1_.refs_2_, f32[24,128]{1,0:T(8,128)S(1)} %get-tuple-element.48.refs_2_.refs_3_, ...), custom_call_target="tpu_custom_call" | custom-call | tf_op jit(solution)/shard_map/finish/pallas_call | solution.py:315
  (3 shorter events, 0.1 us)
Async XLA Ops:
  0.6 0.9 copy-start
  1.6 5.7 %collective-permute-start.2 = (bf16[1,96,256]{2,1,0:T(8,128)(2,1)S(1)}, bf16[1,96,256]{2,1,0:T(8,128)(2,1)S(1)}, u32[]{:S(2)}, u32[]{:S(2)}) collective-permute-start(bf16[1,96,256]{2,1,0:T(8,128)(2,1)S(1)} %dynamic-slice_bitcast_fusion), channel_id=1, source_target_pairs={{0,24},{1,25},{2,26},{3,27},{4,28},{5,29},{6,30},{7,31},{8,16},{9,... | collective-permute-start | bytes 147464 | tf_op jit(solution)/shard_map/ppermute | solution.py:28
  5.7 4.4 %collective-permute-start.1 = (bf16[1,96,256]{2,1,0:T(8,128)(2,1)S(1)}, bf16[1,96,256]{2,1,0:T(8,128)(2,1)S(1)}, u32[]{:S(2)}, u32[]{:S(2)}) collective-permute-start(bf16[1,96,256]{2,1,0:T(8,128)(2,1)S(1)} %dynamic-slice_bitcast_fusion), channel_id=1, source_target_pairs={{0,16},{1,17},{2,18},{3,19},{4,20},{5,21},{6,22},{7,23},{8,24},{9,... | collective-permute-start | bytes 147464 | tf_op jit(solution)/shard_map/ppermute | solution.py:28
  5.7 4.4 %collective-permute-start = (bf16[1,96,256]{2,1,0:T(8,128)(2,1)S(1)}, bf16[1,96,256]{2,1,0:T(8,128)(2,1)S(1)}, u32[]{:S(2)}, u32[]{:S(2)}) collective-permute-start(bf16[1,96,256]{2,1,0:T(8,128)(2,1)S(1)} %dynamic-slice_bitcast_fusion), channel_id=1, source_target_pairs={{0,8},{1,9},{2,10},{3,11},{4,12},{5,13},{6,14},{7,15},{8,0},{9,1},... | collective-permute-start | bytes 147464 | tf_op jit(solution)/shard_map/ppermute | solution.py:28
  10.1 4.3 %collective-permute-start.6 = (bf16[1,4,96,256]{3,2,1,0:T(8,128)(2,1)S(1)}, bf16[1,4,96,256]{3,2,1,0:T(8,128)(2,1)S(1)}, u32[]{:S(2)}, u32[]{:S(2)}) collective-permute-start(bf16[1,4,96,256]{3,2,1,0:T(8,128)(2,1)S(1)} %maximum_bitcast_fusion.refs_3_.refs_7_), channel_id=1, source_target_pairs={{0,1},{1,0},{2,3},{3,2},{4,5},{5,4},{6,7},{7,6},{8,9},{9,8},{10,11... | collective-permute-start | bytes 589832 | tf_op jit(solution)/shard_map/ppermute | solution.py:28
  11.8 7.0 %collective-permute-start.5 = (bf16[1,4,96,256]{3,2,1,0:T(8,128)(2,1)S(1)}, bf16[1,4,96,256]{3,2,1,0:T(8,128)(2,1)S(1)}, u32[]{:S(2)}, u32[]{:S(2)}) collective-permute-start(bf16[1,4,96,256]{3,2,1,0:T(8,128)(2,1)S(1)} %maximum_bitcast_fusion.refs_3_.refs_7_), channel_id=1, source_target_pairs={{0,4},{1,5},{2,6},{3,7},{4,0},{5,1},{6,2},{7,3},{8,12},{9,13},{10,... | collective-permute-start | bytes 589832 | tf_op jit(solution)/shard_map/ppermute | solution.py:28
  13.0 6.1 %collective-permute-start.4 = (bf16[1,4,96,256]{3,2,1,0:T(8,128)(2,1)S(1)}, bf16[1,4,96,256]{3,2,1,0:T(8,128)(2,1)S(1)}, u32[]{:S(2)}, u32[]{:S(2)}) collective-permute-start(bf16[1,4,96,256]{3,2,1,0:T(8,128)(2,1)S(1)} %maximum_bitcast_fusion.refs_3_.refs_7_), channel_id=1, source_target_pairs={{0,2},{1,3},{2,0},{3,1},{4,6},{5,7},{6,4},{7,5},{8,10},{9,11},{10,... | collective-permute-start | bytes 589832 | tf_op jit(solution)/shard_map/ppermute | solution.py:28
  14.2 9.4 %collective-permute-start.3 = (bf16[1,4,96,256]{3,2,1,0:T(8,128)(2,1)S(1)}, bf16[1,4,96,256]{3,2,1,0:T(8,128)(2,1)S(1)}, u32[]{:S(2)}, u32[]{:S(2)}) collective-permute-start(bf16[1,4,96,256]{3,2,1,0:T(8,128)(2,1)S(1)} %maximum_bitcast_fusion.refs_3_.refs_7_), channel_id=1, source_target_pairs={{0,6},{1,7},{2,4},{3,5},{4,2},{5,3},{6,0},{7,1},{8,14},{9,15},{10,... | collective-permute-start | bytes 589832 | tf_op jit(solution)/shard_map/ppermute | solution.py:28
  14.4 1.2 %copy-start.1 = (bf16[2048,256]{1,0:T(8,128)(2,1)S(1)}, bf16[2048,256]{1,0:T(8,128)(2,1)}, u32[]{:S(2)}) copy-start(bf16[2048,256]{1,0:T(8,128)(2,1)} %refs_6_.1) | copy-start | bytes 3145732
  15.7 0.7 copy-start.3
  21.6 4.3 %collective-permute-start.8 = (bf16[1,4,96,256]{3,2,1,0:T(8,128)(2,1)S(1)}, bf16[1,4,96,256]{3,2,1,0:T(8,128)(2,1)S(1)}, u32[]{:S(2)}, u32[]{:S(2)}) collective-permute-start(bf16[1,4,96,256]{3,2,1,0:T(8,128)(2,1)S(1)} %get-tuple-element.35.refs_8_), channel_id=1, source_target_pairs={{0,1},{1,0},{2,3},{3,2},{4,5},{5,4},{6,7},{7,6},{8,9},{9,8},{10,11... | collective-permute-start | bytes 589832 | tf_op jit(solution)/shard_map/ppermute | solution.py:28
  23.6 2.3 %collective-permute-start.9 = (bf16[1,4,96,256]{3,2,1,0:T(8,128)(2,1)S(1)}, bf16[1,4,96,256]{3,2,1,0:T(8,128)(2,1)S(1)}, u32[]{:S(2)}, u32[]{:S(2)}) collective-permute-start(bf16[1,4,96,256]{3,2,1,0:T(8,128)(2,1)S(1)} %get-tuple-element.36.refs_9_), channel_id=1, source_target_pairs={{0,1},{1,0},{2,3},{3,2},{4,5},{5,4},{6,7},{7,6},{8,9},{9,8},{10,11... | collective-permute-start | bytes 589832 | tf_op jit(solution)/shard_map/ppermute | solution.py:28
  24.9 3.3 %collective-permute-start.7 = (bf16[1,4,96,256]{3,2,1,0:T(8,128)(2,1)S(1)}, bf16[1,4,96,256]{3,2,1,0:T(8,128)(2,1)S(1)}, u32[]{:S(2)}, u32[]{:S(2)}) collective-permute-start(bf16[1,4,96,256]{3,2,1,0:T(8,128)(2,1)S(1)} %get-tuple-element.34.refs_10_), channel_id=1, source_target_pairs={{0,1},{1,0},{2,3},{3,2},{4,5},{5,4},{6,7},{7,6},{8,9},{9,8},{10,11... | collective-permute-start | bytes 589832 | tf_op jit(solution)/shard_map/ppermute | solution.py:28
  29.6 1.2 %collective-permute-start.10 = (f32[27,128]{1,0:T(8,128)S(1)}, f32[27,128]{1,0:T(8,128)S(1)}, u32[]{:S(2)}, u32[]{:S(2)}) collective-permute-start(f32[27,128]{1,0:T(8,128)S(1)} %get-tuple-element.43.own_ref), channel_id=1, source_target_pairs={{0,1},{1,0},{2,3},{3,2},{4,5},{5,4},{6,7},{7,6},{8,9},{9,8},{10,11... | collective-permute-start | bytes 41480 | tf_op jit(solution)/shard_map/ppermute | solution.py:28
  61.8 30.6 %copy-start.2 = (bf16[2048,256]{1,0:T(8,128)(2,1)S(1)}, bf16[2048,256]{1,0:T(8,128)(2,1)}, u32[]{:S(2)}) copy-start(bf16[2048,256]{1,0:T(8,128)(2,1)} %refs_6_.1) | copy-start | bytes 3145732
